TPU v7x, 128 devices: a whole 4x4x4 slice. The times are simulated.
128 devices in a mesh: expert: 8 (over x, core), fsdp: 16 (over z, y).
Axes of the slice: x: 4, y: 4, z: 4, core: 2. Of those that a mesh axis runs over, the one named last changes fastest.
Arguments:
- tokens: bfloat16 [16384, 1536], P(('expert', 'fsdp')), may hold values from -6 to 6
- gate_probs: float32 [16384, 2], P(('expert', 'fsdp')), may hold values from 0.1 to 1
- expert_ids: int32 [16384, 2], P(('expert', 'fsdp')), may hold values from 0 to 7, all different within a row; in each aligned block of 128 rows (0 to 127, 128 to 255, ...) at most 32 rows name the same one
- cotangent: bfloat16 [16384, 1536], P(('expert', 'fsdp')), may hold values from -0.59765625 to 0.59765625
- gate_weight: bfloat16 [8, 1536, 2048], P('expert', None, 'fsdp'), may hold values from -0.15625 to 0.15625
- up_weight: bfloat16 [8, 1536, 2048], P('expert', None, 'fsdp'), may hold values from -0.15625 to 0.15625
- down_weight: bfloat16 [8, 2048, 1536], P('expert', 'fsdp'), may hold values from -0.125 to 0.125
Outputs:
- mixed: bfloat16 [16384, 1536], P(('expert', 'fsdp'))
- d_tokens: bfloat16 [16384, 1536], P(('expert', 'fsdp'))
- d_gates: float32 [16384, 2], P(('expert', 'fsdp'))
- d_gate_weight: float32 [8, 1536, 2048], P('expert', None, 'fsdp')
- d_up_weight: float32 [8, 1536, 2048], P('expert', None, 'fsdp')
- d_down_weight: float32 [8, 2048, 1536], P('expert', 'fsdp')
Inputs may be any that keep to these rules, and one draw needn't show every extreme that they name: `expert_ids`: the two experts of a token differ. In the 128 rows of one device every expert is named exactly 32 times.
All inputs are finite; a program needn't handle non-finite values.
Results may differ from a plain program's by a relative error of at most 0.015.
Values may be sent and summed in bfloat16 or wider, within the bound.
A program may use at most 192 MiB of HBM per device.

v0:
```python
import jax
import jax.numpy as jnp
from jax import lax
from jax.sharding import PartitionSpec as P


def build_dispatch(expert_ids, capacity, num_experts):
    flat_ids = expert_ids.reshape(-1)
    onehot = (flat_ids[:, None] == jnp.arange(num_experts, dtype=jnp.int32)[None, :]).astype(
        jnp.int32
    )
    before = jnp.cumsum(onehot, axis=0) - onehot
    slot_pos = jnp.sum(before * onehot, axis=1)
    target = flat_ids * capacity + slot_pos
    return (jnp.arange(num_experts * capacity, dtype=jnp.int32)[:, None] == target[None, :]).astype(
        jnp.bfloat16
    )


def deliver(buffer):
    arrived = lax.all_to_all(buffer, "expert", split_axis=0, concat_axis=0, tiled=True)
    arrived = lax.all_gather(arrived[None], "fsdp", axis=0, tiled=True)
    return arrived.reshape(-1, buffer.shape[-1])


def bring_back(partial_value, num_experts, capacity):
    columns = partial_value.shape[-1]
    blocks = partial_value.astype(jnp.bfloat16).reshape(-1, num_experts, capacity, columns)
    summed = lax.psum_scatter(blocks, "fsdp", scatter_dimension=0, tiled=True).astype(jnp.float32)
    result = lax.all_to_all(
        summed[0].astype(jnp.bfloat16), "expert", split_axis=0, concat_axis=0, tiled=True
    )
    return result.reshape(num_experts * capacity, columns)


def per_device(tokens, gate_probs, expert_ids, cotangent, gate_weight, up_weight, down_weight):
    tok_rows, columns = tokens.shape
    num_experts = lax.axis_size("expert")
    capacity = 2 * tok_rows // num_experts
    dispatch = build_dispatch(expert_ids, capacity, num_experts)
    token_map = jnp.sum(dispatch.reshape(num_experts * capacity, tok_rows, 2), axis=2)
    contract_rows = (((0,), (0,)), ((), ()))
    contract_cols = (((1,), (1,)), ((), ()))
    outgoing = jnp.dot(token_map, tokens, preferred_element_type=jnp.float32).astype(jnp.bfloat16)
    cot_wide = cotangent.astype(jnp.float32)
    scaled = (
        (gate_probs[:, :, None] * cot_wide[:, None, :])
        .astype(jnp.bfloat16)
        .reshape(2 * tok_rows, columns)
    )
    grad_out = jnp.dot(dispatch, scaled, preferred_element_type=jnp.float32).astype(jnp.bfloat16)
    token_slots = outgoing.reshape(num_experts, capacity, columns)
    grad_slots = grad_out.reshape(num_experts, capacity, columns)
    rows_in = deliver(token_slots)
    w_gate = gate_weight[0]
    w_up = up_weight[0]
    w_down = down_weight[0]
    pre_gate = jnp.dot(rows_in, w_gate, preferred_element_type=jnp.float32)
    pre_up = jnp.dot(rows_in, w_up, preferred_element_type=jnp.float32)
    sigmoid_gate = jax.nn.sigmoid(pre_gate)
    hidden = (pre_gate * sigmoid_gate * pre_up).astype(jnp.bfloat16)
    partial_value = jnp.dot(hidden, w_down, preferred_element_type=jnp.float32)
    expert_out = bring_back(partial_value, num_experts, capacity)
    per_pair = lax.dot_general(
        dispatch, expert_out, contract_rows, preferred_element_type=jnp.float32
    ).reshape(tok_rows, 2, columns)
    mixed = jnp.sum(gate_probs[:, :, None] * per_pair, axis=1).astype(jnp.bfloat16)
    d_gates = jnp.sum(cot_wide[:, None, :] * per_pair, axis=2)
    grad_rows = deliver(grad_slots)
    d_hidden = lax.dot_general(grad_rows, w_down, contract_cols, preferred_element_type=jnp.float32)
    d_pre_gate = (
        d_hidden * pre_up * sigmoid_gate * (1.0 + pre_gate * (1.0 - sigmoid_gate))
    ).astype(jnp.bfloat16)
    d_pre_up = (d_hidden * pre_gate * sigmoid_gate).astype(jnp.bfloat16)
    d_down = lax.dot_general(hidden, grad_rows, contract_rows, preferred_element_type=jnp.float32)
    d_gate_w = lax.dot_general(
        rows_in, d_pre_gate, contract_rows, preferred_element_type=jnp.float32
    )
    d_up_w = lax.dot_general(rows_in, d_pre_up, contract_rows, preferred_element_type=jnp.float32)
    back_partial = lax.dot_general(
        d_pre_gate, w_gate, contract_cols, preferred_element_type=jnp.float32
    )
    back_partial = back_partial + lax.dot_general(
        d_pre_up, w_up, contract_cols, preferred_element_type=jnp.float32
    )
    d_rows = bring_back(back_partial, num_experts, capacity)
    d_tokens = lax.dot_general(
        token_map, d_rows, contract_rows, preferred_element_type=jnp.float32
    ).astype(jnp.bfloat16)
    return (mixed, d_tokens, d_gates, d_gate_w[None], d_up_w[None], d_down[None])


def solution(mesh):
    placed = (
        P(("expert", "fsdp"), None),
        P(("expert", "fsdp"), None),
        P(("expert", "fsdp"), None),
        P(("expert", "fsdp"), None),
        P("expert", None, "fsdp"),
        P("expert", None, "fsdp"),
        P("expert", "fsdp", None),
    )
    return jax.shard_map(
        per_device,
        mesh=mesh,
        in_specs=placed,
        out_specs=(
            P(("expert", "fsdp"), None),
            P(("expert", "fsdp"), None),
            P(("expert", "fsdp"), None),
            P("expert", None, "fsdp"),
            P("expert", None, "fsdp"),
            P("expert", "fsdp", None),
        ),
        check_vma=False,
    )
```

profile of v0, /device:TPU:1, one launch (start us, length us, event | category | flops | bytes accessed | tf_op | source)
XLA Modules:
  0.0 466.0 jit_solution(14920518914551212987)
XLA Ops:
  7.2 0.0 all-gather.5.cloned.1.call-start
  7.2 0.9 copy.36
  8.1 0.1 reshape.107
  8.3 0.1 eq.62
  8.4 0.6 reduce-window.6
  9.0 0.2 slice_reduce_fusion
  9.3 0.1 fusion.17
  9.4 0.1 reduce_sum.42
  9.5 0.1 copy.38
  9.6 0.7 multiply_add_fusion
  10.3 0.6 copy-done.9
  10.9 1.3 convolution_convert_fusion.1
  12.3 17.8 %all_to_all.20 = bf16[8,32,1536]{2,1,0:T(8,128)(2,1)} all-to-all(bf16[8,32,1536]{2,1,0:T(8,128)(2,1)S(1)} %bitcast.70), channel_id=1, replica_groups=mesh['expert'=8,'fsdp'=16] {'expert'}, dimensions={0} | all-to-all | bytes 1572864 | tf_op jit(solution)/shard_map/all_to_all | solution.py:21
  30.1 0.0 all-gather.5.cloned.1.call-update
  30.1 0.0 all-gather.7.cloned.1.call-start
  30.2 0.1 copy.40
  30.3 0.1 mul.83
  30.5 0.4 mul.85.clone
  30.9 1.1 mul.86
  32.0 0.5 convolution_convert_fusion.2
  32.5 16.3 %all_to_all.21 = bf16[8,32,1536]{2,1,0:T(8,128)(2,1)} all-to-all(bf16[8,32,1536]{2,1,0:T(8,128)(2,1)S(1)} %bitcast.71), channel_id=1, replica_groups=mesh['expert'=8,'fsdp'=16] {'expert'}, dimensions={0} | all-to-all | bytes 1572864 | tf_op jit(solution)/shard_map/all_to_all | solution.py:21
  48.7 0.0 all-gather.7.cloned.1.call-update
  48.7 0.2 reduce-scatter.9.cloned.1.call-start
  49.0 72.0 %all-gather.5.cloned.1.call-done = bf16[128,32,1536]{2,1,0:T(8,128)(2,1)} async-done(((bf16[8,32,1536]{2,1,0:T(8,128)(2,1)}), bf16[128,32,1536]{2,1,0:T(8,128)(2,1)}) %all-gather.5.cloned.1.call-update) | async-done | bytes 12582928 | tf_op jit(solution)/shard_map/all_gather | solution.py:22
  120.9 7.9 %fusion.5 = f32[4096,128]{1,0:T(8,128)} fusion(bf16[4096,1536]{1,0:T(8,128)(2,1)} %bitcast.63, bf16[1,1536,128]{2,1,0:T(8,128)(2,1)S(1)} %copy-done.2), kind=kOutput, calls=%fused_computation.20 | convolution fusion | flops 1610612736 | bytes 15073280 | tf_op jit(solution)/shard_map/dot_general | solution.py:59
  128.8 1.1 copy-done.1
  129.9 4.8 %fusion.9 = f32[4096,128]{1,0:T(8,128)} fusion(bf16[4096,1536]{1,0:T(8,128)(2,1)S(1)} %bitcast.66, bf16[1,1536,128]{2,1,0:T(8,128)(2,1)S(1)} %copy-done.5), kind=kOutput, calls=%fused_computation.24 | convolution fusion | flops 1610612736 | bytes 15073280 | tf_op jit(solution)/shard_map/dot_general | solution.py:58
  134.6 78.0 %all-gather.7.cloned.1.call-done = bf16[128,32,1536]{2,1,0:T(8,128)(2,1)} async-done(((bf16[8,32,1536]{2,1,0:T(8,128)(2,1)}), bf16[128,32,1536]{2,1,0:T(8,128)(2,1)}) %all-gather.7.cloned.1.call-update) | async-done | bytes 12582928 | tf_op jit(solution)/shard_map/all_gather | solution.py:22
  212.6 9.6 %multiply_convert_fusion = (bf16[4096,128]{1,0:T(8,128)(2,1)S(1)}, bf16[4096,128]{1,0:T(8,128)(2,1)S(1)}, bf16[4096,128]{1,0:T(8,128)(2,1)S(1)}) fusion(f32[4096,128]{1,0:T(8,128)} %fusion.9, f32[4096,128]{1,0:T(8,128)} %fusion.5, bf16[4096,1536]{1,0:T(8,128)(2,1)} %bitcast.67, bf16[1,128,1536]{2,1,0:T(8,128)(2,1)S(1)} %copy-done), kind=kOutput, calls=%fused_computation.8 | convolution fusion | flops 1619001344 | bytes 20316160 | tf_op jit(solution)/shard_map/dot_general | solution.py:70
  222.2 10.1 %fusion.7 = f32[4096,1536]{1,0:T(8,128)} fusion(bf16[4096,128]{1,0:T(8,128)(2,1)S(1)} %get-tuple-element.9, bf16[1,1536,128]{2,1,0:T(8,128)(2,1)S(1)} %copy-done.5), kind=kOutput, calls=%fused_computation.22 | convolution fusion | flops 1610612736 | bytes 26607616 | tf_op jit(solution)/shard_map/dot_general | solution.py:80
  232.4 14.7 %add_convert_fusion = bf16[4096,1536]{1,0:T(8,128)(2,1)} fusion(f32[4096,1536]{1,0:T(8,128)} %fusion.7, bf16[4096,128]{1,0:T(8,128)(2,1)S(1)} %get-tuple-element.8, bf16[1,1536,128]{2,1,0:T(8,128)(2,1)S(1)} %copy-done.2), kind=kOutput, calls=%fused_computation | convolution fusion | flops 1623195648 | bytes 39190528 | tf_op jit(solution)/shard_map/dot_general | solution.py:83
  247.1 0.0 reduce-scatter.9.cloned.1.call-update
  247.1 0.3 reduce-scatter.7.cloned.1.call-start
  247.4 6.4 %convolution_convert_fusion = bf16[4096,1536]{1,0:T(8,128)(2,1)} fusion(bf16[4096,128]{1,0:T(8,128)(2,1)S(1)} %get-tuple-element.10, bf16[1,128,1536]{2,1,0:T(8,128)(2,1)S(1)} %copy-done), kind=kOutput, calls=%fused_computation.1 | convolution fusion | flops 1616904192 | bytes 14024704 | tf_op jit(solution)/shard_map/dot_general | solution.py:62
  253.7 1.0 copy-done.4
  254.7 1.0 convert_element_type.65
  255.7 0.1 iota_compare_fusion.2
  255.8 0.7 eq.68
  256.5 7.5 %convolution_bitcast_fusion.1 = f32[1,1536,128]{2,1,0:T(8,128)} fusion(bf16[4096,1536]{1,0:T(8,128)(2,1)} %bitcast.64, bf16[4096,128]{1,0:T(8,128)(2,1)S(1)} %get-tuple-element.8), kind=kOutput, calls=%fused_computation.5 | convolution fusion | flops 1610612736 | bytes 14417920 | tf_op jit(solution)/shard_map/dot_general | solution.py:79
  264.0 77.9 %reduce-scatter.9.cloned.1.call-done = bf16[1,8,32,1536]{3,2,1,0:T(8,128)(2,1)} async-done(((bf16[16,8,32,1536]{3,2,1,0:T(8,128)(2,1)}), bf16[1,8,32,1536]{3,2,1,0:T(8,128)(2,1)}) %reduce-scatter.9.cloned.1.call-update) | async-done | bytes 786448
  341.9 5.4 %all-to-all-start.3 = ((bf16[8,32,1536]{2,1,0:T(8,128)(2,1)}), bf16[8,32,1536]{2,1,0:T(8,128)(2,1)S(1)}, u32[]{:S(2)}, u32[]{:S(2)}) async-start(bf16[8,32,1536]{2,1,0:T(8,128)(2,1)} %bitcast.73), calls=%async_computation.3 | async-start | bytes 1572864 | tf_op jit(solution)/shard_map/all_to_all | solution.py:30
  347.3 7.3 %convolution_bitcast_fusion.2 = f32[1,1536,128]{2,1,0:T(8,128)} fusion(bf16[4096,1536]{1,0:T(8,128)(2,1)} %bitcast.65, bf16[4096,128]{1,0:T(8,128)(2,1)S(1)} %copy-done.7), kind=kOutput, calls=%fused_computation.6 | convolution fusion | flops 1610612736 | bytes 14417920 | tf_op jit(solution)/shard_map/dot_general | solution.py:76
  354.6 84.7 %reduce-scatter.7.cloned.1.call-done = bf16[1,8,32,1536]{3,2,1,0:T(8,128)(2,1)} async-done(((bf16[16,8,32,1536]{3,2,1,0:T(8,128)(2,1)}), bf16[1,8,32,1536]{3,2,1,0:T(8,128)(2,1)}) %reduce-scatter.7.cloned.1.call-update) | async-done | bytes 786448
  439.4 5.4 %all-to-all-start.1 = ((bf16[8,32,1536]{2,1,0:T(8,128)(2,1)}), bf16[8,32,1536]{2,1,0:T(8,128)(2,1)}, u32[]{:S(2)}, u32[]{:S(2)}) async-start(bf16[8,32,1536]{2,1,0:T(8,128)(2,1)} %bitcast.72), calls=%async_computation.1 | async-start | bytes 1572864 | tf_op jit(solution)/shard_map/all_to_all | solution.py:30
  444.8 7.4 %convolution_bitcast_fusion = f32[1,128,1536]{2,1,0:T(8,128)} fusion(bf16[4096,128]{1,0:T(8,128)(2,1)S(1)} %get-tuple-element.10, bf16[4096,1536]{1,0:T(8,128)(2,1)} %bitcast.68), kind=kOutput, calls=%fused_computation.4 | convolution fusion | flops 1610612736 | bytes 14417920 | tf_op jit(solution)/shard_map/dot_general | solution.py:75
  452.2 1.0 convolution_convert_fusion.3
  453.2 3.8 all-to-all-done.1
  457.0 2.5 multiply_reduce_fusion
  (30 shorter events, 0.2 us)
Async XLA Ops:
  7.2 205.4 %copy-start = (bf16[1,128,1536]{2,1,0:T(8,128)(2,1)S(1)}, bf16[1,128,1536]{2,1,0:T(8,128)(2,1)}, u32[]{:S(2)}) copy-start(bf16[1,128,1536]{2,1,0:T(8,128)(2,1)} %param.13) | copy-start | bytes 1179652
  7.2 23.0 %copy-start.12 = (f32[128,2]{0,1:T(2,128)S(1)}, f32[128,2]{0,1:T(2,128)}, u32[]{:S(2)}) copy-start(f32[128,2]{0,1:T(2,128)} %param.8) | copy-start | bytes 3076
  7.2 23.3 %copy-start.3 = (bf16[128,1536]{1,0:T(8,128)(2,1)S(1)}, bf16[128,1536]{1,0:T(8,128)(2,1)}, u32[]{:S(2)}) copy-start(bf16[128,1536]{1,0:T(8,128)(2,1)} %param.10) | copy-start | bytes 1179652
  7.2 113.7 %all-gather.5.cloned.1.call-start = ((), (), s32[]{:S(2)}) async-start(), calls=%async_computation.6 | async-start | bytes 13369344 | tf_op jit(solution)/shard_map/all_gather | solution.py:22
  10.3 0.6 copy-start.9
  30.1 182.5 %all-gather.7.cloned.1.call-start = ((), (), s32[]{:S(2)}) async-start(), calls=%async_computation.7 | async-start | bytes 13369344 | tf_op jit(solution)/shard_map/all_gather | solution.py:22
  32.0 89.0 %copy-start.2 = (bf16[1,1536,128]{2,1,0:T(8,128)(2,1)S(1)}, bf16[1,1536,128]{2,1,0:T(8,128)(2,1)}, u32[]{:S(2)}) copy-start(bf16[1,1536,128]{2,1,0:T(8,128)(2,1)} %param.12) | copy-start | bytes 1179652
  48.7 293.1 %reduce-scatter.9.cloned.1.call-start = ((), (), s32[]{:S(2)}) async-start(), calls=%async_computation.9 | async-start | bytes 13369344
  120.9 8.9 %copy-start.1 = (bf16[128,32,1536]{2,1,0:T(8,128)(2,1)S(1)}, bf16[128,32,1536]{2,1,0:T(8,128)(2,1)}, u32[]{:S(2)}) copy-start(bf16[128,32,1536]{2,1,0:T(8,128)(2,1)} %all-gather.5.cloned.1.call-done) | copy-start | bytes 37748740
  120.9 8.9 %copy-start.5 = (bf16[1,1536,128]{2,1,0:T(8,128)(2,1)S(1)}, bf16[1,1536,128]{2,1,0:T(8,128)(2,1)}, u32[]{:S(2)}) copy-start(bf16[1,1536,128]{2,1,0:T(8,128)(2,1)} %param.11) | copy-start | bytes 1179652
  222.2 10.1 %copy-start.6 = (bf16[4096,128]{1,0:T(8,128)(2,1)}, bf16[4096,128]{1,0:T(8,128)(2,1)S(1)}, u32[]{:S(2)}) copy-start(bf16[4096,128]{1,0:T(8,128)(2,1)S(1)} %get-tuple-element.9) | copy-start | bytes 3145732
  247.1 192.3 %reduce-scatter.7.cloned.1.call-start = ((), (), s32[]{:S(2)}) async-start(), calls=%async_computation.8 | async-start | bytes 13369344
  253.7 1.0 copy-start.4
  256.5 90.8 %copy-start.7 = (bf16[4096,128]{1,0:T(8,128)(2,1)S(1)}, bf16[4096,128]{1,0:T(8,128)(2,1)}, u32[]{:S(2)}) copy-start(bf16[4096,128]{1,0:T(8,128)(2,1)} %copy-done.6) | copy-start | bytes 3145732
  341.9 97.5 %all-to-all-start.3 = ((bf16[8,32,1536]{2,1,0:T(8,128)(2,1)}), bf16[8,32,1536]{2,1,0:T(8,128)(2,1)S(1)}, u32[]{:S(2)}, u32[]{:S(2)}) async-start(bf16[8,32,1536]{2,1,0:T(8,128)(2,1)} %bitcast.73), calls=%async_computation.3 | async-start | bytes 1572864 | tf_op jit(solution)/shard_map/all_to_all | solution.py:30
  439.4 17.7 %all-to-all-start.1 = ((bf16[8,32,1536]{2,1,0:T(8,128)(2,1)}), bf16[8,32,1536]{2,1,0:T(8,128)(2,1)}, u32[]{:S(2)}, u32[]{:S(2)}) async-start(bf16[8,32,1536]{2,1,0:T(8,128)(2,1)} %bitcast.72), calls=%async_computation.1 | async-start | bytes 1572864 | tf_op jit(solution)/shard_map/all_to_all | solution.py:30
  444.8 7.4 %copy-start.10 = (bf16[256,128]{1,0:T(8,128)(2,1)S(1)}, bf16[256,128]{1,0:T(8,128)(2,1)}, u32[]{:S(2)}) copy-start(bf16[256,128]{1,0:T(8,128)(2,1)} %copy-done.9) | copy-start | bytes 196612
  444.8 12.3 %copy-start.8 = (f32[128,1536]{1,0:T(8,128)S(1)}, f32[128,1536]{1,0:T(8,128)}, u32[]{:S(2)}) copy-start(f32[128,1536]{1,0:T(8,128)} %convert_element_type.65) | copy-start | bytes 2359300
  444.8 12.3 %copy-start.11 = (pred[128,2,256]{2,1,0:T(4,128)(4,1)S(1)}, pred[128,2,256]{2,1,0:T(4,128)(4,1)}, u32[]{:S(2)}) copy-start(pred[128,2,256]{2,1,0:T(4,128)(4,1)} %eq.68) | copy-start | bytes 196612
Sparse Core Ops, SparseCore 0:
  30.3 90.6 all-gather.4
  123.1 89.4 all-gather.6
  247.2 94.6 reduce-scatter.8
  345.2 94.1 reduce-scatter.6
where the time goes:
time: 467 us; the launch traced here: 466 us
  waiting for transfers between devices  316 us (68%)
  matrix products  81 us (17%)
  blocking collectives  34.1 us (7%)
  between operations  13.9 us (3%)
  starting transfers between devices  11.4 us (2%)
  local copies, waits for them, and re-layouts  6.75 us (1%)
    unnamed x6, waiting for transfers between devices  163 us
    all_gather x2, waiting for transfers between devices, deliver(): arrived = lax.all_gather(arrived[None], 'fsdp', axis=0, tiled=True)  150 us
    all_to_all x2, blocking collectives, deliver(): lax.all_to_all(buffer, 'expert', split_axis=0, concat_axis=0, tiled=True)  34.1 us
    dot_general x1, matrix products, per_device(): lax.dot_general(d_pre_up, w_up, contract_cols, preferred_element_type=jnp...  14.7 us
    all_to_all x2, starting transfers between devices, bring_back(): lax.all_to_all(summed[0].astype(jnp.bfloat16), 'expert', split_axis=0, co...  10.8 us
    dot_general x1, matrix products, per_device(): lax.dot_general(d_pre_gate, w_gate, contract_cols, preferred_element_type...  10.1 us
    dot_general x1, matrix products, per_device(): lax.dot_general(grad_rows, w_down, contract_cols, preferred_element_type=...  9.6 us
  transfers between devices with their start and end apart: 6, of which 5 were waited for; matrix products, arithmetic and copies ran while one was open for 10% of the time, Pallas kernels for 0%

commit v1 on v0

v1 whole, which is shorter than its diff:
```python
import functools

import jax
import jax.numpy as jnp
from jax import lax
from jax.experimental import pallas as pl
from jax.experimental.pallas import tpu as pltpu
from jax.sharding import PartitionSpec as P

MESH = pl.DeviceIdType.MESH
F32, BF16 = jnp.float32, jnp.bfloat16
RING = 4
ROWS_ROWS = (((0,), (0,)), ((), ()))
COLS_COLS = (((1,), (1,)), ((), ()))


def layer_kernel(
    n_exp,
    tok_ref, gp_ref, ids_ref, cot_ref, wg_ref, wu_ref, wd_ref,
    mixed_ref, dtok_ref, dgate_ref, dwg_ref, dwu_ref, dwd_ref,
    x_buf, g_buf, wg_buf, wu_buf, wd_buf, x_send, g_send,
    a_buf, b_buf, h_buf, ht_buf, dp_buf, dpt_buf,
    p_out, p_back, p_gu, p_dn,
    via_out, via_back, via_gu, via_dn,
    in_out, in_back, in_gu, in_dn,
    own_out, own_back, own_gu, own_dn,
    out_send, back_send, out_home, back_home,
    send_sem, recv_sem,
):
    tok, d = tok_ref.shape
    cap = 2 * tok // n_exp
    rows = n_exp * cap
    hs = wg_ref.shape[1]
    half = rows // 2
    tile = min(256, d)
    n_tiles = d // tile

    me = lax.axis_index("expert")
    f = lax.axis_index("fsdp")
    core = me % 2
    z, y = f // RING, f % RING
    along_z_up, along_z_down = ((z + 1) % RING) * RING + y, ((z + 3) % RING) * RING + y
    along_y_up, along_y_down = z * RING + (y + 1) % RING, z * RING + (y + 3) % RING
    t_right = along_z_up * (1 - core) + along_y_up * core
    t_left = along_z_down * (1 - core) + along_y_down * core
    w_right = along_y_up * (1 - core) + along_z_up * core
    w_left = along_y_down * (1 - core) + along_z_down * core
    tr, tl = {"fsdp": t_right}, {"fsdp": t_left}
    wr, wl = {"fsdp": w_right}, {"fsdp": w_left}

    barrier = pltpu.get_barrier_semaphore()
    for dev in (tr, tl, wr, wl):
        pl.semaphore_signal(barrier, inc=1, device_id=dev, device_id_type=MESH)
    for k in range(1, n_exp):
        pl.semaphore_signal(
            barrier, inc=1, device_id={"expert": (me + k) % n_exp}, device_id_type=MESH
        )

    started = []
    counter = [0]

    def ids(n):
        first = counter[0]
        counter[0] += n
        return first

    def copy(src, dst, n, dev):
        return pltpu.make_async_remote_copy(
            src_ref=src, dst_ref=dst, send_sem=send_sem.at[n], recv_sem=recv_sem.at[n],
            device_id=dev, device_id_type=MESH,
        )

    def send(src, dst, n, dev):
        c = copy(src, dst, n, dev)
        c.start()
        started.append(c)
        return c

    class Gather:
        def __init__(self, own, slot, halves, right, left):
            self.own, self.slot, self.halves = own, slot, halves
            self.right, self.left = right, left
            self.n = ids(4)

        def start(self):
            self.r = send(self.own, self.slot(1), self.n, self.right)
            self.l = send(self.own, self.slot(3), self.n + 1, self.left)

        def relay(self):
            lo, hi = self.halves
            self.r.wait_recv()
            self.rr = send(lo(self.slot(1)), lo(self.slot(2)), self.n + 2, self.right)
            self.l.wait_recv()
            self.ll = send(hi(self.slot(3)), hi(self.slot(2)), self.n + 3, self.left)

        def finish(self):
            self.rr.wait_recv()
            self.ll.wait_recv()

    class Scatter:
        def __init__(self, part, via, arrived, right, left):
            self.part, self.via, self.arrived = part, via, arrived
            self.right, self.left = right, left
            self.n = ids(6)

        def far(self):
            self.a = send(self.part.at[1, 0], self.via.at[0], self.n, self.right)
            self.b = send(self.part.at[1, 1], self.via.at[1], self.n + 1, self.left)

        def near(self):
            self.c = send(self.part.at[2, 1], self.arrived.at[0, 1], self.n + 2, self.right)
            self.d = send(self.part.at[0, 0], self.arrived.at[1, 0], self.n + 3, self.left)

        def add(self):
            def plus(slot, h):
                total = self.part[slot, h].astype(F32) + self.via[h].astype(F32)
                self.part[slot, h] = total.astype(BF16)

            self.a.wait_recv()
            plus(2, 0)
            self.e = send(self.part.at[2, 0], self.arrived.at[0, 0], self.n + 4, self.right)
            self.b.wait_recv()
            plus(0, 1)
            self.g = send(self.part.at[0, 1], self.arrived.at[1, 1], self.n + 5, self.left)

        def finish(self):
            for c in (self.c, self.d, self.e, self.g):
                c.wait_recv()

    class Exchange:
        def __init__(self, src, slot):
            self.src, self.slot = src, slot
            self.n = ids(n_exp - 1)

        def start(self):
            self.copies = [
                send(
                    self.src.at[(me + k) % n_exp], self.slot(me), self.n + k - 1,
                    {"expert": (me + k) % n_exp},
                )
                for k in range(1, n_exp)
            ]

        def finish(self):
            for c in self.copies:
                c.wait_recv()

    def w_rows(ref, lo, n):
        return ref.at[pl.ds(lo, n), :]

    whole_d, whole_h = d // 2, hs // 2
    gather_wg = Gather(
        wg_ref, lambda s: wg_buf.at[s - 1],
        (lambda r: w_rows(r, 0, whole_d), lambda r: w_rows(r, whole_d, whole_d)), wr, wl,
    )
    gather_wu = Gather(
        wu_ref, lambda s: wu_buf.at[s - 1],
        (lambda r: w_rows(r, 0, whole_d), lambda r: w_rows(r, whole_d, whole_d)), wr, wl,
    )
    gather_wd = Gather(
        wd_ref, lambda s: wd_buf.at[s - 1],
        (lambda r: w_rows(r, 0, whole_h), lambda r: w_rows(r, whole_h, whole_h)), wr, wl,
    )
    experts_half = n_exp // 2
    row_halves = (
        lambda r: r.at[pl.ds(0, experts_half)],
        lambda r: r.at[pl.ds(experts_half, experts_half)],
    )
    gather_x = Gather(x_buf.at[0], lambda s: x_buf.at[s], row_halves, tr, tl)
    gather_g = Gather(g_buf.at[0], lambda s: g_buf.at[s], row_halves, tr, tl)
    deal_x = Exchange(x_send, lambda e: x_buf.at[0, e])
    deal_g = Exchange(g_send, lambda e: g_buf.at[0, e])
    scatter_out = Scatter(p_out, via_out, in_out, tr, tl)
    scatter_back = Scatter(p_back, via_back, in_back, tr, tl)
    scatter_gu = Scatter(p_gu, via_gu, in_gu, wr, wl)
    scatter_dn = Scatter(p_dn, via_dn, in_dn, wr, wl)
    home_out = Exchange(out_send, lambda e: out_home.at[e])
    home_back = Exchange(back_send, lambda e: back_home.at[e])

    lane = lax.broadcasted_iota(jnp.int32, (tok, rows), 1)
    expert_of, slot_of = lane // cap, lane % cap
    named = [ids_ref[:, k : k + 1] == expert_of for k in range(2)]
    either = (named[0] | named[1]).astype(F32).astype(BF16)
    earlier = (
        lax.broadcasted_iota(jnp.int32, (tok, tok), 1)
        < lax.broadcasted_iota(jnp.int32, (tok, tok), 0)
    ).astype(F32).astype(BF16)
    before = jnp.dot(earlier, either, preferred_element_type=F32)
    here = before == slot_of.astype(F32)
    pick = [(named[k] & here).astype(F32).astype(BF16) for k in range(2)]
    pick_any = pick[0] + pick[1]

    pl.semaphore_wait(barrier, 4 + n_exp - 1)
    gather_wg.start()
    gather_wu.start()
    gather_wd.start()

    def cols(n):
        return pl.ds(pl.multiple_of(n * tile, tile), tile)

    def deal_tile(n, _):
        c = cols(n)
        sent = lax.dot_general(pick_any, tok_ref[:, c], ROWS_ROWS, preferred_element_type=F32)
        x_send[:, :, c] = sent.astype(BF16).reshape(n_exp, cap, tile)
        return 0

    lax.fori_loop(0, n_tiles, deal_tile, 0)
    deal_x.start()
    x_buf[0, me] = x_send[me]

    def deal_grad_tile(n, _):
        c = cols(n)
        cot = cot_ref[:, c].astype(F32)
        sent = sum(
            lax.dot_general(
                pick[k], (gp_ref[:, k : k + 1] * cot).astype(BF16), ROWS_ROWS,
                preferred_element_type=F32,
            )
            for k in range(2)
        )
        g_send[:, :, c] = sent.astype(BF16).reshape(n_exp, cap, tile)
        return 0

    lax.fori_loop(0, n_tiles, deal_grad_tile, 0)
    deal_g.start()
    g_buf[0, me] = g_send[me]

    wg = [wg_ref] + [wg_buf.at[s] for s in range(3)]
    wu = [wu_ref] + [wu_buf.at[s] for s in range(3)]
    wd = [wd_ref] + [wd_buf.at[s] for s in range(3)]

    gather_wg.relay()
    gather_wu.relay()
    deal_x.finish()
    gather_x.start()
    gather_wd.relay()
    deal_g.finish()
    gather_g.start()

    def forward(i):
        x = x_buf[i].reshape(rows, d)
        for j in range(RING):
            w = jnp.concatenate([wg[j][...], wu[j][...]], axis=1)
            pre = jnp.dot(x, w, preferred_element_type=F32)
            g, u = pre[:, :hs], pre[:, hs:]
            s = 1.0 / (1.0 + jnp.exp(-g))
            gs = g * s
            c = slice(j * hs, (j + 1) * hs)
            h = (gs * u).astype(BF16)
            h_buf[i, :, c] = h
            a_buf[i, :, c] = u * s * (1.0 + g * (1.0 - s))
            b_buf[i, :, c] = gs
            ht_buf[c, pl.ds(pl.multiple_of(i * rows, rows), rows)] = h.T

    def backward(i):
        g = g_buf[i].reshape(rows, d)
        for j in range(0, RING, 2):
            w = jnp.concatenate([wd[j][...], wd[j + 1][...]], axis=0)
            dh = lax.dot_general(g, w, COLS_COLS, preferred_element_type=F32)
            for jj in range(2):
                c = slice((j + jj) * hs, (j + jj + 1) * hs)
                part = dh[:, jj * hs : (jj + 1) * hs]
                dp = jnp.concatenate([part * a_buf[i, :, c], part * b_buf[i, :, c]], axis=1)
                dp = dp.astype(BF16)
                dp_buf[i, :, (j + jj) * 2 * hs : (j + jj + 1) * 2 * hs] = dp
                dpt_buf[j + jj, :, pl.ds(pl.multiple_of(i * rows, rows), rows)] = dp.T

    def store_rows(part, own, slot, c, value):
        if slot == 0:
            own[:, c] = value
        else:
            n = value.shape[0] // 2
            part[slot - 1, 0, :, c] = value[:n].astype(BF16)
            part[slot - 1, 1, :, c] = value[n:].astype(BF16)

    def out_part(i):
        def one(n, _):
            c = cols(n)
            w = jnp.concatenate([wd[j][:, c] for j in range(RING)], axis=0)
            store_rows(p_out, own_out, i, c, jnp.dot(h_buf[i], w, preferred_element_type=F32))
            return 0

        lax.fori_loop(0, n_tiles, one, 0)

    def back_part(i):
        def one(n, _):
            c = cols(n)
            w = jnp.concatenate(
                [r[c, :] for j in range(RING) for r in (wg[j], wu[j])], axis=1
            )
            value = lax.dot_general(dp_buf[i], w, COLS_COLS, preferred_element_type=F32)
            store_rows(p_back, own_back, i, c, value)
            return 0

        lax.fori_loop(0, n_tiles, one, 0)

    def gate_up_part(j):
        def one(n, _):
            c = cols(n)
            x = x_buf[:, :, :, c].reshape(RING * rows, tile)
            store_rows(p_gu, own_gu, j, c, jnp.dot(dpt_buf[j], x, preferred_element_type=F32))
            return 0

        lax.fori_loop(0, n_tiles, one, 0)

    def down_parts():
        def one(n, _):
            c = cols(n)
            g = g_buf[:, :, :, c].reshape(RING * rows, tile)
            value = jnp.dot(ht_buf[...], g, preferred_element_type=F32)
            for j in range(RING):
                store_rows(p_dn, own_dn, j, c, value[j * hs : (j + 1) * hs])
            return 0

        lax.fori_loop(0, n_tiles, one, 0)

    def three(body):
        def step(k, _):
            body(k + k // 2)
            return 0

        lax.fori_loop(0, 3, step, 0)

    gather_x.relay()
    gather_wg.finish()
    gather_wu.finish()
    three(forward)
    gather_x.finish()
    forward(2)
    gather_wd.finish()
    out_part(2)
    scatter_out.far()
    gather_g.relay()
    out_part(1)
    out_part(3)
    scatter_out.near()
    scatter_out.add()
    out_part(0)

    three(backward)
    gather_g.finish()
    backward(2)
    back_part(2)
    scatter_back.far()
    back_part(1)
    back_part(3)
    scatter_back.near()

    def total(arrived, own, sent):
        for h in range(2):
            value = (
                own[h * half : (h + 1) * half, :]
                + arrived[0, h].astype(F32)
                + arrived[1, h].astype(F32)
            )
            sent[h * experts_half : (h + 1) * experts_half] = value.astype(BF16).reshape(
                experts_half, cap, d
            )

    scatter_out.finish()
    total(in_out, own_out, out_send)
    home_out.start()
    out_home[me] = out_send[me]

    scatter_back.add()
    back_part(0)
    down_parts()
    scatter_dn.far()
    scatter_dn.near()
    gate_up_part(2)
    scatter_gu.far()
    scatter_dn.add()
    gate_up_part(1)
    gate_up_part(3)
    scatter_gu.near()
    scatter_back.finish()
    total(in_back, own_back, back_send)
    home_back.start()
    back_home[me] = back_send[me]
    scatter_gu.add()
    gate_up_part(0)

    home_out.finish()
    column = lax.broadcasted_iota(jnp.int32, (tok, 2), 1)

    def mix_tile(n, inner):
        c = cols(n)
        home = out_home[:, :, c].reshape(rows, tile)
        per = [jnp.dot(pick[k], home, preferred_element_type=F32) for k in range(2)]
        mixed_ref[:, c] = (gp_ref[:, 0:1] * per[0] + gp_ref[:, 1:2] * per[1]).astype(BF16)
        cot = cot_ref[:, c].astype(F32)
        return tuple(
            inner[k] + jnp.sum(cot * per[k], axis=1, keepdims=True) for k in range(2)
        )

    zero = jnp.zeros((tok, 1), F32)
    inner = lax.fori_loop(0, n_tiles, mix_tile, (zero, zero))
    dgate_ref[...] = jnp.where(column == 0, inner[0], inner[1])

    scatter_dn.finish()
    for h in range(2):
        r = slice(h * hs // 2, (h + 1) * hs // 2)
        dwd_ref[r, :] = own_dn[r, :] + in_dn[0, h].astype(F32) + in_dn[1, h].astype(F32)

    home_back.finish()

    def home_tile(n, _):
        c = cols(n)
        home = back_home[:, :, c].reshape(rows, tile)
        dtok_ref[:, c] = jnp.dot(pick_any, home, preferred_element_type=F32).astype(BF16)
        return 0

    lax.fori_loop(0, n_tiles, home_tile, 0)

    scatter_gu.finish()
    for h, ref in enumerate((dwg_ref, dwu_ref)):
        value = (
            own_gu[h * hs : (h + 1) * hs, :]
            + in_gu[0, h].astype(F32)
            + in_gu[1, h].astype(F32)
        )
        ref[...] = value.T

    for c in started:
        c.wait_send()


def per_device(tokens, gate_probs, expert_ids, cotangent, gate_weight, up_weight, down_weight):
    tok, d = tokens.shape
    n_exp = lax.axis_size("expert")
    cap = 2 * tok // n_exp
    rows = 2 * tok
    hs = gate_weight.shape[2]
    hidden = RING * hs
    n_copies = 4 * 5 + 6 * 4 + 4 * (n_exp - 1)
    vmem = pltpu.VMEM
    shapes = [
        vmem((RING, n_exp, cap, d), BF16),
        vmem((RING, n_exp, cap, d), BF16),
        vmem((3, d, hs), BF16),
        vmem((3, d, hs), BF16),
        vmem((3, hs, d), BF16),
        vmem((n_exp, cap, d), BF16),
        vmem((n_exp, cap, d), BF16),
        vmem((RING, rows, hidden), F32),
        vmem((RING, rows, hidden), F32),
        vmem((RING, rows, hidden), BF16),
        vmem((hidden, RING * rows), BF16),
        vmem((RING, rows, 2 * hidden), BF16),
        vmem((RING, 2 * hs, RING * rows), BF16),
    ]
    heights = (rows, rows, 2 * hs, hs)
    shapes += [vmem((3, 2, n // 2, d), BF16) for n in heights]
    shapes += [vmem((2, n // 2, d), BF16) for n in heights]
    shapes += [vmem((2, 2, n // 2, d), BF16) for n in heights]
    shapes += [vmem((n, d), F32) for n in heights]
    shapes += [vmem((n_exp, cap, d), BF16) for _ in range(4)]
    shapes += [pltpu.SemaphoreType.DMA((n_copies,)), pltpu.SemaphoreType.DMA((n_copies,))]
    spec = pl.BlockSpec(memory_space=pltpu.VMEM)
    outs = pl.pallas_call(
        functools.partial(layer_kernel, n_exp),
        out_shape=[
            jax.ShapeDtypeStruct((tok, d), BF16),
            jax.ShapeDtypeStruct((tok, d), BF16),
            jax.ShapeDtypeStruct((tok, 2), F32),
            jax.ShapeDtypeStruct((d, hs), F32),
            jax.ShapeDtypeStruct((d, hs), F32),
            jax.ShapeDtypeStruct((hs, d), F32),
        ],
        in_specs=[spec] * 7,
        out_specs=[spec] * 6,
        scratch_shapes=shapes,
        compiler_params=pltpu.CompilerParams(
            collective_id=0, has_side_effects=True, vmem_limit_bytes=63 * 1024 * 1024
        ),
    )(
        tokens, gate_probs, expert_ids, cotangent,
        gate_weight[0], up_weight[0], down_weight[0],
    )
    mixed, d_tokens, d_gates, d_gate_w, d_up_w, d_down = outs
    return mixed, d_tokens, d_gates, d_gate_w[None], d_up_w[None], d_down[None]


def solution(mesh):
    rows = P(("expert", "fsdp"), None)
    hidden = P("expert", None, "fsdp")
    hidden_rows = P("expert", "fsdp", None)
    return jax.shard_map(
        per_device,
        mesh=mesh,
        in_specs=(rows, rows, rows, rows, hidden, hidden, hidden_rows),
        out_specs=(rows, rows, rows, hidden, hidden, hidden_rows),
        check_vma=False,
    )
```

time: 467 us -> 119 us (0.25)
  waiting for transfers between devices: 316 us -> 0 us
  Pallas kernels: 0 us -> 108 us
  matrix products: 81 us -> 0 us
  blocking collectives: 34.1 us -> 0 us
  between operations: 13.9 us -> 0.66 us
  starting transfers between devices: 11.4 us -> 0 us
    unnamed x6 -> x0, waiting for transfers between devices: 163 us -> none
    all_gather x2 -> x0, waiting for transfers between devices: 150 us -> none  [deliver(): arrived = lax.all_gather(arrived[None], 'fsdp', axis=0, tiled=True)]
    pallas_call x0 -> x1, Pallas kernels: none -> 108 us  [per_device(): pl.pallas_call(functools.partial(layer_kernel, n_exp), out_shape=[jax.Sha...]
    dot_general x13 -> x0, matrix products: 81 us -> none  [the longest x1 14.7 us: per_device(): lax.dot_general(d_pre_up, w_up, contract_cols, preferred_element_type=jnp...]
    all_to_all x2 -> x0, blocking collectives: 34.1 us -> none  [deliver(): lax.all_to_all(buffer, 'expert', split_axis=0, concat_axis=0, tiled=True)]
    all_to_all x2 -> x0, starting transfers between devices: 10.8 us -> none  [bring_back(): lax.all_to_all(summed[0].astype(jnp.bfloat16), 'expert', split_axis=0, co...]
    unnamed x28 -> x20, local copies, waits for them, and re-layouts: 3.7 us -> 9.99 us
  transfers between devices with their start and end apart: 6 -> 0, of which waited for: 5 -> 0; matrix products, arithmetic and copies ran while one was open for 10% -> 0% of each run, Pallas kernels for 0% -> 0%
where the time goes in v1:
time: 119 us; the launch traced here: 118 us
  Pallas kernels  108 us (91%)
  local copies, waits for them, and re-layouts  9.99 us (8%)
    pallas_call x1, Pallas kernels, per_device(): pl.pallas_call(functools.partial(layer_kernel, n_exp), out_shape=[jax.Sha...  108 us
    unnamed x20, local copies, waits for them, and re-layouts  9.99 us

profile of v1, /device:TPU:1, one launch (start us, length us, event | category | flops | bytes accessed | tf_op | source)
XLA Modules:
  0.0 118.3 jit_solution(8340869814854202369)
XLA Ops:
  0.6 0.0 copy-start.4
  0.6 0.7 copy-done.4
  1.3 0.0 copy-start.5
  1.3 0.7 copy.13.gp_ref
  2.1 0.0 copy-done.5
  2.1 0.7 copy.14.ids_ref
  2.8 107.6 %shard_map.118 = (bf16[128,1536]{1,0:T(8,128)(2,1)}, bf16[128,1536]{1,0:T(8,128)(2,1)}, f32[128,2]{1,0:T(8,128)}, f32[1536,128]{1,0:T(8,128)}, f32[1536,128]{1,0:T(8,128)}, /*index=5*/f32[128,1536]{1,0:T(8,128)}) custom-call(bf16[128,1536]{1,0:T(8,128)(2,1)} %tok_ref.1, f32[128,2]{1,0:T(8,128)} %copy.13.gp_ref, s32[128,2]{1,0:T(8,128)} %copy.14.ids_ref, ...), custom_call_target="tpu_custom_call" | custom-call | tf_op jit(solution)/shard_map/pallas_call | solution.py:460
  110.4 0.0 copy-start.3
  110.4 1.5 %copy.15 = f32[128,2]{0,1:T(2,128)} copy(f32[128,2]{1,0:T(8,128)} %get-tuple-element.20) | data formatting | bytes 2048
  111.9 0.0 copy-start.2
  111.9 1.8 %copy.21 = bf16[128,1536]{1,0:T(8,128)(2,1)} copy(bf16[128,1536]{1,0:T(8,128)(2,1)} %get-tuple-element.30) | data formatting | bytes 786432
  113.8 0.0 copy-done.3
  113.8 0.7 copy.22
  114.5 0.0 copy-done.2
  114.5 0.0 copy-start.1
  114.5 0.9 copy.23
  115.4 0.5 copy-done.1
  116.0 0.0 copy-start
  116.0 0.9 copy.24
  116.8 0.5 copy-done
  117.4 0.9 copy.25
Async XLA Ops:
  0.6 0.7 copy-start.4
  1.3 0.7 copy-start.5
  110.4 3.4 %copy-start.3 = (bf16[128,1536]{1,0:T(8,128)(2,1)S(1)}, bf16[128,1536]{1,0:T(8,128)(2,1)}, u32[]{:S(2)}) copy-start(bf16[128,1536]{1,0:T(8,128)(2,1)} %get-tuple-element.31) | copy-start | bytes 1179652
  111.9 2.6 %copy-start.2 = (f32[1536,128]{1,0:T(8,128)S(1)}, f32[1536,128]{1,0:T(8,128)}, u32[]{:S(2)}) copy-start(f32[1536,128]{1,0:T(8,128)} %get-tuple-element.15) | copy-start | bytes 2359300
  114.5 1.4 %copy-start.1 = (f32[1536,128]{1,0:T(8,128)S(1)}, f32[1536,128]{1,0:T(8,128)}, u32[]{:S(2)}) copy-start(f32[1536,128]{1,0:T(8,128)} %get-tuple-element.16) | copy-start | bytes 2359300
  116.0 1.4 %copy-start = (f32[128,1536]{1,0:T(8,128)S(1)}, f32[128,1536]{1,0:T(8,128)}, u32[]{:S(2)}) copy-start(f32[128,1536]{1,0:T(8,128)} %get-tuple-element.17) | copy-start | bytes 2359300

commit v2 on v1

--- a/solution.py
+++ b/solution.py
@@ -16,16 +16,16 @@
 
 def layer_kernel(
     n_exp,
-    tok_ref, gp_ref, ids_ref, cot_ref, wg_ref, wu_ref, wd_ref,
+    tok_hbm, gp_ref, ids_ref, cot_hbm, wg_ref, wu_ref, wd_ref,
     mixed_ref, dtok_ref, dgate_ref, dwg_ref, dwu_ref, dwd_ref,
-    x_buf, g_buf, wg_buf, wu_buf, wd_buf, x_send, g_send,
+    tok_ref, cot_ref, x_buf, g_buf, wg_buf, wu_buf, wd_buf, x_send, g_send,
     a_buf, b_buf, h_buf, ht_buf, dp_buf, dpt_buf,
     p_out, p_back, p_gu, p_dn,
     via_out, via_back, via_gu, via_dn,
     in_out, in_back, in_gu, in_dn,
     own_out, own_back, own_gu, own_dn,
     out_send, back_send, out_home, back_home,
-    send_sem, recv_sem,
+    send_sem, recv_sem, load_sem,
 ):
     tok, d = tok_ref.shape
     cap = 2 * tok // n_exp
@@ -56,6 +56,18 @@
             barrier, inc=1, device_id={"expert": (me + k) % n_exp}, device_id_type=MESH
         )
 
+    loads = [
+        pltpu.make_async_copy(src, dst, load_sem.at[n])
+        for n, (src, dst) in enumerate(
+            [
+                (tok_hbm, tok_ref), (cot_hbm, cot_ref),
+                (wg_ref, wg_buf.at[0]), (wu_ref, wu_buf.at[0]), (wd_ref, wd_buf.at[0]),
+            ]
+        )
+    ]
+    for load in loads:
+        load.start()
+
     started = []
     counter = [0]
 
@@ -80,18 +92,26 @@
         def __init__(self, own, slot, halves, right, left):
             self.own, self.slot, self.halves = own, slot, halves
             self.right, self.left = right, left
-            self.n = ids(4)
+            self.n = ids(6)
 
         def start(self):
-            self.r = send(self.own, self.slot(1), self.n, self.right)
-            self.l = send(self.own, self.slot(3), self.n + 1, self.left)
+            lo, hi = self.halves
+            near, far, n = self.slot(1), self.slot(3), self.n
+            self.r_lo = send(lo(self.own), lo(near), n, self.right)
+            self.l_hi = send(hi(self.own), hi(far), n + 1, self.left)
+            self.r_hi = send(hi(self.own), hi(near), n + 2, self.right)
+            self.l_lo = send(lo(self.own), lo(far), n + 3, self.left)
 
         def relay(self):
             lo, hi = self.halves
-            self.r.wait_recv()
-            self.rr = send(lo(self.slot(1)), lo(self.slot(2)), self.n + 2, self.right)
-            self.l.wait_recv()
-            self.ll = send(hi(self.slot(3)), hi(self.slot(2)), self.n + 3, self.left)
+            self.r_lo.wait_recv()
+            self.rr = send(lo(self.slot(1)), lo(self.slot(2)), self.n + 4, self.right)
+            self.l_hi.wait_recv()
+            self.ll = send(hi(self.slot(3)), hi(self.slot(2)), self.n + 5, self.left)
+
+        def sides(self):
+            self.r_hi.wait_recv()
+            self.l_lo.wait_recv()
 
         def finish(self):
             self.rr.wait_recv()
@@ -150,15 +170,15 @@
 
     whole_d, whole_h = d // 2, hs // 2
     gather_wg = Gather(
-        wg_ref, lambda s: wg_buf.at[s - 1],
+        wg_ref, lambda s: wg_buf.at[s],
         (lambda r: w_rows(r, 0, whole_d), lambda r: w_rows(r, whole_d, whole_d)), wr, wl,
     )
     gather_wu = Gather(
-        wu_ref, lambda s: wu_buf.at[s - 1],
+        wu_ref, lambda s: wu_buf.at[s],
         (lambda r: w_rows(r, 0, whole_d), lambda r: w_rows(r, whole_d, whole_d)), wr, wl,
     )
     gather_wd = Gather(
-        wd_ref, lambda s: wd_buf.at[s - 1],
+        wd_ref, lambda s: wd_buf.at[s],
         (lambda r: w_rows(r, 0, whole_h), lambda r: w_rows(r, whole_h, whole_h)), wr, wl,
     )
     experts_half = n_exp // 2
@@ -179,12 +199,21 @@
 
     lane = lax.broadcasted_iota(jnp.int32, (tok, rows), 1)
     expert_of, slot_of = lane // cap, lane % cap
-    named = [ids_ref[:, k : k + 1] == expert_of for k in range(2)]
+    token = lax.broadcasted_iota(jnp.int32, (tok, tok), 0)
+    other = lax.broadcasted_iota(jnp.int32, (tok, tok), 1)
+
+    def column_of(row):
+        return jnp.sum(jnp.where(token == other, row, 0.0), axis=1, keepdims=True)
+
+    def row_of(column):
+        return jnp.sum(jnp.where(token == other, column, 0.0), axis=0, keepdims=True)
+
+    gates = [column_of(gp_ref[k : k + 1, :]) for k in range(2)]
+    choices = ids_ref[...].astype(F32)
+    chosen = expert_of.astype(F32)
+    named = [column_of(choices[k : k + 1, :]) == chosen for k in range(2)]
     either = (named[0] | named[1]).astype(F32).astype(BF16)
-    earlier = (
-        lax.broadcasted_iota(jnp.int32, (tok, tok), 1)
-        < lax.broadcasted_iota(jnp.int32, (tok, tok), 0)
-    ).astype(F32).astype(BF16)
+    earlier = (other < token).astype(F32).astype(BF16)
     before = jnp.dot(earlier, either, preferred_element_type=F32)
     here = before == slot_of.astype(F32)
     pick = [(named[k] & here).astype(F32).astype(BF16) for k in range(2)]
@@ -204,6 +233,7 @@
         x_send[:, :, c] = sent.astype(BF16).reshape(n_exp, cap, tile)
         return 0
 
+    loads[0].wait()
     lax.fori_loop(0, n_tiles, deal_tile, 0)
     deal_x.start()
     x_buf[0, me] = x_send[me]
@@ -213,7 +243,7 @@
         cot = cot_ref[:, c].astype(F32)
         sent = sum(
             lax.dot_general(
-                pick[k], (gp_ref[:, k : k + 1] * cot).astype(BF16), ROWS_ROWS,
+                pick[k], (gates[k] * cot).astype(BF16), ROWS_ROWS,
                 preferred_element_type=F32,
             )
             for k in range(2)
@@ -221,13 +251,14 @@
         g_send[:, :, c] = sent.astype(BF16).reshape(n_exp, cap, tile)
         return 0
 
+    loads[1].wait()
     lax.fori_loop(0, n_tiles, deal_grad_tile, 0)
     deal_g.start()
     g_buf[0, me] = g_send[me]
 
-    wg = [wg_ref] + [wg_buf.at[s] for s in range(3)]
-    wu = [wu_ref] + [wu_buf.at[s] for s in range(3)]
-    wd = [wd_ref] + [wd_buf.at[s] for s in range(3)]
+    wg = [wg_buf.at[s] for s in range(RING)]
+    wu = [wu_buf.at[s] for s in range(RING)]
+    wd = [wd_buf.at[s] for s in range(RING)]
 
     gather_wg.relay()
     gather_wu.relay()
@@ -235,6 +266,7 @@
     gather_x.start()
     gather_wd.relay()
     deal_g.finish()
+    gather_x.relay()
     gather_g.start()
 
     def forward(i):
@@ -314,37 +346,12 @@
 
         lax.fori_loop(0, n_tiles, one, 0)
 
-    def three(body):
+    def both_sides(body):
         def step(k, _):
-            body(k + k // 2)
+            body(1 + 2 * k)
             return 0
 
-        lax.fori_loop(0, 3, step, 0)
-
-    gather_x.relay()
-    gather_wg.finish()
-    gather_wu.finish()
-    three(forward)
-    gather_x.finish()
-    forward(2)
-    gather_wd.finish()
-    out_part(2)
-    scatter_out.far()
-    gather_g.relay()
-    out_part(1)
-    out_part(3)
-    scatter_out.near()
-    scatter_out.add()
-    out_part(0)
-
-    three(backward)
-    gather_g.finish()
-    backward(2)
-    back_part(2)
-    scatter_back.far()
-    back_part(1)
-    back_part(3)
-    scatter_back.near()
+        lax.fori_loop(0, 2, step, 0)
 
     def total(arrived, own, sent):
         for h in range(2):
@@ -357,22 +364,52 @@
                 experts_half, cap, d
             )
 
+    for load in loads[2:]:
+        load.wait()
+    for gather in (gather_wg, gather_wu):
+        gather.sides()
+        gather.finish()
+    forward(0)
+    gather_x.sides()
+    both_sides(forward)
+    gather_x.finish()
+    forward(2)
+    gather_g.relay()
+    gather_wd.sides()
+    gather_wd.finish()
+    out_part(2)
+    scatter_out.far()
+    out_part(1)
+    out_part(3)
+    scatter_out.near()
+    out_part(0)
+
+    backward(0)
+    gather_g.sides()
+    both_sides(backward)
+    scatter_out.add()
+    gather_g.finish()
+    backward(2)
+    back_part(2)
+    scatter_back.far()
+    back_part(1)
+    back_part(3)
+    scatter_back.near()
     scatter_out.finish()
     total(in_out, own_out, out_send)
     home_out.start()
     out_home[me] = out_send[me]
-
+    down_parts()
     scatter_back.add()
-    back_part(0)
-    down_parts()
     scatter_dn.far()
     scatter_dn.near()
     gate_up_part(2)
     scatter_gu.far()
-    scatter_dn.add()
+    back_part(0)
     gate_up_part(1)
     gate_up_part(3)
     scatter_gu.near()
+    scatter_dn.add()
     scatter_back.finish()
     total(in_back, own_back, back_send)
     home_back.start()
@@ -381,13 +418,12 @@
     gate_up_part(0)
 
     home_out.finish()
-    column = lax.broadcasted_iota(jnp.int32, (tok, 2), 1)
 
     def mix_tile(n, inner):
         c = cols(n)
         home = out_home[:, :, c].reshape(rows, tile)
         per = [jnp.dot(pick[k], home, preferred_element_type=F32) for k in range(2)]
-        mixed_ref[:, c] = (gp_ref[:, 0:1] * per[0] + gp_ref[:, 1:2] * per[1]).astype(BF16)
+        mixed_ref[:, c] = (gates[0] * per[0] + gates[1] * per[1]).astype(BF16)
         cot = cot_ref[:, c].astype(F32)
         return tuple(
             inner[k] + jnp.sum(cot * per[k], axis=1, keepdims=True) for k in range(2)
@@ -395,7 +431,8 @@
 
     zero = jnp.zeros((tok, 1), F32)
     inner = lax.fori_loop(0, n_tiles, mix_tile, (zero, zero))
-    dgate_ref[...] = jnp.where(column == 0, inner[0], inner[1])
+    for k in range(2):
+        dgate_ref[k : k + 1, :] = row_of(inner[k])
 
     scatter_dn.finish()
     for h in range(2):
@@ -425,6 +462,16 @@
         c.wait_send()
 
 
+def write_kernel(*refs):
+    n = len(refs) // 2
+    sem = refs[-1]
+    copies = [pltpu.make_async_copy(refs[k], refs[n + k], sem.at[k]) for k in range(n)]
+    for c in copies:
+        c.start()
+    for c in copies:
+        c.wait()
+
+
 def per_device(tokens, gate_probs, expert_ids, cotangent, gate_weight, up_weight, down_weight):
     tok, d = tokens.shape
     n_exp = lax.axis_size("expert")
@@ -432,14 +479,16 @@
     rows = 2 * tok
     hs = gate_weight.shape[2]
     hidden = RING * hs
-    n_copies = 4 * 5 + 6 * 4 + 4 * (n_exp - 1)
+    n_copies = 6 * 5 + 6 * 4 + 4 * (n_exp - 1)
     vmem = pltpu.VMEM
     shapes = [
+        vmem((tok, d), BF16),
+        vmem((tok, d), BF16),
         vmem((RING, n_exp, cap, d), BF16),
         vmem((RING, n_exp, cap, d), BF16),
-        vmem((3, d, hs), BF16),
-        vmem((3, d, hs), BF16),
-        vmem((3, hs, d), BF16),
+        vmem((RING, d, hs), BF16),
+        vmem((RING, d, hs), BF16),
+        vmem((RING, hs, d), BF16),
         vmem((n_exp, cap, d), BF16),
         vmem((n_exp, cap, d), BF16),
         vmem((RING, rows, hidden), F32),
@@ -455,30 +504,34 @@
     shapes += [vmem((2, 2, n // 2, d), BF16) for n in heights]
     shapes += [vmem((n, d), F32) for n in heights]
     shapes += [vmem((n_exp, cap, d), BF16) for _ in range(4)]
-    shapes += [pltpu.SemaphoreType.DMA((n_copies,)), pltpu.SemaphoreType.DMA((n_copies,))]
-    spec = pl.BlockSpec(memory_space=pltpu.VMEM)
-    outs = pl.pallas_call(
+    shapes += [pltpu.SemaphoreType.DMA((n,)) for n in (n_copies, n_copies, 5)]
+    here, away = pl.BlockSpec(memory_space=pltpu.VMEM), pl.BlockSpec(memory_space=pl.ANY)
+    results = [
+        ((tok, d), BF16), ((tok, d), BF16), ((2, tok), F32),
+        ((d, hs), F32), ((d, hs), F32), ((hs, d), F32),
+    ]
+    inside = pl.pallas_call(
         functools.partial(layer_kernel, n_exp),
-        out_shape=[
-            jax.ShapeDtypeStruct((tok, d), BF16),
-            jax.ShapeDtypeStruct((tok, d), BF16),
-            jax.ShapeDtypeStruct((tok, 2), F32),
-            jax.ShapeDtypeStruct((d, hs), F32),
-            jax.ShapeDtypeStruct((d, hs), F32),
-            jax.ShapeDtypeStruct((hs, d), F32),
-        ],
-        in_specs=[spec] * 7,
-        out_specs=[spec] * 6,
+        out_shape=[pltpu.VMEM(*r) for r in results],
+        in_specs=[away, here, here, away, away, away, away],
+        out_specs=[here] * len(results),
         scratch_shapes=shapes,
         compiler_params=pltpu.CompilerParams(
-            collective_id=0, has_side_effects=True, vmem_limit_bytes=63 * 1024 * 1024
+            collective_id=0, has_side_effects=True, vmem_limit_bytes=58 * 1024 * 1024
         ),
     )(
-        tokens, gate_probs, expert_ids, cotangent,
+        tokens, gate_probs.T, expert_ids.T, cotangent,
         gate_weight[0], up_weight[0], down_weight[0],
     )
-    mixed, d_tokens, d_gates, d_gate_w, d_up_w, d_down = outs
-    return mixed, d_tokens, d_gates, d_gate_w[None], d_up_w[None], d_down[None]
+    mixed, d_tokens, d_gates, d_gate_w, d_up_w, d_down = pl.pallas_call(
+        write_kernel,
+        out_shape=[jax.ShapeDtypeStruct(*r) for r in results],
+        in_specs=[here] * len(results),
+        out_specs=[away] * len(results),
+        scratch_shapes=[pltpu.SemaphoreType.DMA((len(results),))],
+        compiler_params=pltpu.CompilerParams(vmem_limit_bytes=1024 * 1024),
+    )(*inside)
+    return mixed, d_tokens, d_gates.T, d_gate_w[None], d_up_w[None], d_down[None]
 
 
 def solution(mesh):

time: 119 us -> 103 us (0.87)
  local copies, waits for them, and re-layouts: 9.99 us -> 0 us
  Pallas kernels: 108 us -> 102 us
    unnamed x20 -> x0, local copies, waits for them, and re-layouts: 9.99 us -> none
    pallas_call x1 -> x2, Pallas kernels: 108 us -> 102 us  [the longest x1 101 us: per_device(): pl.pallas_call(functools.partial(layer_kernel, n_exp), out_shape=[pltpu.V...]
where the time goes in v2:
time: 103 us
  Pallas kernels  102 us (99%)
    pallas_call x1, Pallas kernels, per_device(): pl.pallas_call(functools.partial(layer_kernel, n_exp), out_shape=[pltpu.V...  101 us

profile of v2, /device:TPU:1, one launch (start us, length us, event | category | flops | bytes accessed | tf_op | source)
XLA Modules:
  0.0 103.1 jit_solution(2990437508022063722)
XLA Ops:
  0.6 100.7 %shard_map.118 = (bf16[128,1536]{1,0:T(8,128)(2,1)S(1)}, bf16[128,1536]{1,0:T(8,128)(2,1)S(1)}, f32[2,128]{1,0:T(2,128)S(1)}, f32[1536,128]{1,0:T(8,128)S(1)}, f...) custom-call(bf16[128,1536]{1,0:T(8,128)(2,1)} %tok_hbm.1, f32[2,128]{1,0:T(2,128)} %bitcast.12, s32[2,128]{1,0:T(2,128)} %bitcast.13, ...), custom_call_target="tpu_custom_call" | custom-call | tf_op jit(solution)/shard_map/pallas_call | solution.py:513
  101.3 1.7 %shard_map.119 = (bf16[128,1536]{1,0:T(8,128)(2,1)}, bf16[128,1536]{1,0:T(8,128)(2,1)}, f32[2,128]{1,0:T(2,128)}, f32[1536,128]{1,0:T(8,128)}, f32[1536,128]{1,0:T(8,128)}, /*index=5*/f32[128,1536]{1,0:T(8,128)}) custom-call(bf16[128,1536]{1,0:T(8,128)(2,1)S(1)} %get-tuple-element.18.refs_0_, bf16[128,1536]{1,0:T(8,128)(2,1)S(1)} %get-tuple-element.19.refs_1_, ...), custom_call_target="tpu_custom_call" | custom-call | tf_op jit(solution)/shard_map/pallas_call | solution.py:526

commit v3 on v2

--- a/solution.py
+++ b/solution.py
@@ -16,9 +16,9 @@
 
 def layer_kernel(
     n_exp,
-    tok_hbm, gp_ref, ids_ref, cot_hbm, wg_ref, wu_ref, wd_ref,
+    tok_hbm, gp_hbm, ids_hbm, cot_hbm, wg_ref, wu_ref, wd_ref,
     mixed_ref, dtok_ref, dgate_ref, dwg_ref, dwu_ref, dwd_ref,
-    tok_ref, cot_ref, x_buf, g_buf, wg_buf, wu_buf, wd_buf, x_send, g_send,
+    tok_ref, cot_ref, gp_ref, ids_ref, x_buf, g_buf, wg_buf, wu_buf, wd_buf, x_send, g_send,
     a_buf, b_buf, h_buf, ht_buf, dp_buf, dpt_buf,
     p_out, p_back, p_gu, p_dn,
     via_out, via_back, via_gu, via_dn,
@@ -60,7 +60,7 @@
         pltpu.make_async_copy(src, dst, load_sem.at[n])
         for n, (src, dst) in enumerate(
             [
-                (tok_hbm, tok_ref), (cot_hbm, cot_ref),
+                (ids_hbm, ids_ref), (gp_hbm, gp_ref), (tok_hbm, tok_ref), (cot_hbm, cot_ref),
                 (wg_ref, wg_buf.at[0]), (wu_ref, wu_buf.at[0]), (wd_ref, wd_buf.at[0]),
             ]
         )
@@ -197,6 +197,13 @@
     home_out = Exchange(out_send, lambda e: out_home.at[e])
     home_back = Exchange(back_send, lambda e: back_home.at[e])
 
+    pl.semaphore_wait(barrier, 4 + n_exp - 1)
+    gather_wg.start()
+    gather_wu.start()
+    gather_wd.start()
+
+    loads[0].wait()
+    loads[1].wait()
     lane = lax.broadcasted_iota(jnp.int32, (tok, rows), 1)
     expert_of, slot_of = lane // cap, lane % cap
     token = lax.broadcasted_iota(jnp.int32, (tok, tok), 0)
@@ -219,11 +226,6 @@
     pick = [(named[k] & here).astype(F32).astype(BF16) for k in range(2)]
     pick_any = pick[0] + pick[1]
 
-    pl.semaphore_wait(barrier, 4 + n_exp - 1)
-    gather_wg.start()
-    gather_wu.start()
-    gather_wd.start()
-
     def cols(n):
         return pl.ds(pl.multiple_of(n * tile, tile), tile)
 
@@ -233,7 +235,7 @@
         x_send[:, :, c] = sent.astype(BF16).reshape(n_exp, cap, tile)
         return 0
 
-    loads[0].wait()
+    loads[2].wait()
     lax.fori_loop(0, n_tiles, deal_tile, 0)
     deal_x.start()
     x_buf[0, me] = x_send[me]
@@ -251,7 +253,7 @@
         g_send[:, :, c] = sent.astype(BF16).reshape(n_exp, cap, tile)
         return 0
 
-    loads[1].wait()
+    loads[3].wait()
     lax.fori_loop(0, n_tiles, deal_grad_tile, 0)
     deal_g.start()
     g_buf[0, me] = g_send[me]
@@ -364,7 +366,7 @@
                 experts_half, cap, d
             )
 
-    for load in loads[2:]:
+    for load in loads[4:]:
         load.wait()
     for gather in (gather_wg, gather_wu):
         gather.sides()
@@ -399,22 +401,21 @@
     total(in_out, own_out, out_send)
     home_out.start()
     out_home[me] = out_send[me]
-    down_parts()
+    gate_up_part(2)
     scatter_back.add()
-    scatter_dn.far()
-    scatter_dn.near()
-    gate_up_part(2)
     scatter_gu.far()
-    back_part(0)
     gate_up_part(1)
     gate_up_part(3)
     scatter_gu.near()
-    scatter_dn.add()
+    down_parts()
+    scatter_dn.far()
+    scatter_dn.near()
+    back_part(0)
+    scatter_gu.add()
     scatter_back.finish()
     total(in_back, own_back, back_send)
     home_back.start()
     back_home[me] = back_send[me]
-    scatter_gu.add()
     gate_up_part(0)
 
     home_out.finish()
@@ -434,11 +435,7 @@
     for k in range(2):
         dgate_ref[k : k + 1, :] = row_of(inner[k])
 
-    scatter_dn.finish()
-    for h in range(2):
-        r = slice(h * hs // 2, (h + 1) * hs // 2)
-        dwd_ref[r, :] = own_dn[r, :] + in_dn[0, h].astype(F32) + in_dn[1, h].astype(F32)
-
+    scatter_dn.add()
     home_back.finish()
 
     def home_tile(n, _):
@@ -457,6 +454,11 @@
             + in_gu[1, h].astype(F32)
         )
         ref[...] = value.T
+
+    scatter_dn.finish()
+    for h in range(2):
+        r = slice(h * hs // 2, (h + 1) * hs // 2)
+        dwd_ref[r, :] = own_dn[r, :] + in_dn[0, h].astype(F32) + in_dn[1, h].astype(F32)
 
     for c in started:
         c.wait_send()
@@ -484,6 +486,8 @@
     shapes = [
         vmem((tok, d), BF16),
         vmem((tok, d), BF16),
+        vmem((2, tok), F32),
+        vmem((2, tok), jnp.int32),
         vmem((RING, n_exp, cap, d), BF16),
         vmem((RING, n_exp, cap, d), BF16),
         vmem((RING, d, hs), BF16),
@@ -504,7 +508,7 @@
     shapes += [vmem((2, 2, n // 2, d), BF16) for n in heights]
     shapes += [vmem((n, d), F32) for n in heights]
     shapes += [vmem((n_exp, cap, d), BF16) for _ in range(4)]
-    shapes += [pltpu.SemaphoreType.DMA((n,)) for n in (n_copies, n_copies, 5)]
+    shapes += [pltpu.SemaphoreType.DMA((n,)) for n in (n_copies, n_copies, 7)]
     here, away = pl.BlockSpec(memory_space=pltpu.VMEM), pl.BlockSpec(memory_space=pl.ANY)
     results = [
         ((tok, d), BF16), ((tok, d), BF16), ((2, tok), F32),
@@ -513,7 +517,7 @@
     inside = pl.pallas_call(
         functools.partial(layer_kernel, n_exp),
         out_shape=[pltpu.VMEM(*r) for r in results],
-        in_specs=[away, here, here, away, away, away, away],
+        in_specs=[away] * 7,
         out_specs=[here] * len(results),
         scratch_shapes=shapes,
         compiler_params=pltpu.CompilerParams(

time: 103 us -> 102 us (level)
  no operation moved by 1% of the time
where the time goes in v3:
time: 102 us
  Pallas kernels  101 us (99%)
    pallas_call x1, Pallas kernels, per_device(): pl.pallas_call(functools.partial(layer_kernel, n_exp), out_shape=[pltpu.V...  99.8 us

profile of v3, /device:TPU:1, one launch (start us, length us, event | category | flops | bytes accessed | tf_op | source)
XLA Modules:
  0.0 102.1 jit_solution(11280482411682388301)
XLA Ops:
  0.6 99.8 %shard_map.118 = (bf16[128,1536]{1,0:T(8,128)(2,1)S(1)}, bf16[128,1536]{1,0:T(8,128)(2,1)S(1)}, f32[2,128]{1,0:T(2,128)S(1)}, f32[1536,128]{1,0:T(8,128)S(1)}, f...) custom-call(bf16[128,1536]{1,0:T(8,128)(2,1)} %tok_hbm.1, f32[2,128]{1,0:T(2,128)} %bitcast.12, s32[2,128]{1,0:T(2,128)} %bitcast.13, ...), custom_call_target="tpu_custom_call" | custom-call | tf_op jit(solution)/shard_map/pallas_call | solution.py:517
  100.4 1.7 %shard_map.119 = (bf16[128,1536]{1,0:T(8,128)(2,1)}, bf16[128,1536]{1,0:T(8,128)(2,1)}, f32[2,128]{1,0:T(2,128)}, f32[1536,128]{1,0:T(8,128)}, f32[1536,128]{1,0:T(8,128)}, /*index=5*/f32[128,1536]{1,0:T(8,128)}) custom-call(bf16[128,1536]{1,0:T(8,128)(2,1)S(1)} %get-tuple-element.18.refs_0_, bf16[128,1536]{1,0:T(8,128)(2,1)S(1)} %get-tuple-element.19.refs_1_, ...), custom_call_target="tpu_custom_call" | custom-call | tf_op jit(solution)/shard_map/pallas_call | solution.py:530

commit v4 on v3

--- a/solution.py
+++ b/solution.py
@@ -68,117 +68,117 @@
     for load in loads:
         load.start()
 
-    started = []
-    counter = [0]
-
-    def ids(n):
-        first = counter[0]
-        counter[0] += n
+    flows = []
+    used = [0, 0]
+
+    def take(which, n):
+        first = used[which]
+        used[which] += n
         return first
 
-    def copy(src, dst, n, dev):
-        return pltpu.make_async_remote_copy(
-            src_ref=src, dst_ref=dst, send_sem=send_sem.at[n], recv_sem=recv_sem.at[n],
-            device_id=dev, device_id_type=MESH,
-        )
-
-    def send(src, dst, n, dev):
-        c = copy(src, dst, n, dev)
-        c.start()
-        started.append(c)
-        return c
-
-    class Gather:
-        def __init__(self, own, slot, halves, right, left):
-            self.own, self.slot, self.halves = own, slot, halves
+    class Flow:
+        def __init__(self, n_recv, bytes_out):
+            self.out, self.into = take(0, 1), take(1, n_recv)
+            self.bytes_out = bytes_out
+            flows.append(self)
+
+        def descriptor(self, src, dst, n, dev):
+            return pltpu.make_async_remote_copy(
+                src_ref=src, dst_ref=dst, send_sem=send_sem.at[self.out],
+                recv_sem=recv_sem.at[self.into + n], device_id=dev, device_id_type=MESH,
+            )
+
+        def send(self, src, dst, n, dev):
+            self.descriptor(src, dst, n, dev).start()
+
+        def arrive(self, ref, n):
+            self.descriptor(ref, ref, n, tr).wait_recv()
+
+        def sent(self):
+            self.descriptor(self.bytes_out, self.bytes_out, 0, tr).wait_send()
+
+    class Gather(Flow):
+        def __init__(self, own, buf, halves, right, left):
+            super().__init__(4, buf.at[pl.ds(1, RING - 1)])
+            self.own, self.slot, self.halves = own, lambda k: buf.at[k], halves
             self.right, self.left = right, left
-            self.n = ids(6)
 
         def start(self):
             lo, hi = self.halves
-            near, far, n = self.slot(1), self.slot(3), self.n
-            self.r_lo = send(lo(self.own), lo(near), n, self.right)
-            self.l_hi = send(hi(self.own), hi(far), n + 1, self.left)
-            self.r_hi = send(hi(self.own), hi(near), n + 2, self.right)
-            self.l_lo = send(lo(self.own), lo(far), n + 3, self.left)
+            self.send(lo(self.own), lo(self.slot(1)), 0, self.right)
+            self.send(hi(self.own), hi(self.slot(3)), 1, self.left)
+            self.send(hi(self.own), hi(self.slot(1)), 2, self.right)
+            self.send(lo(self.own), lo(self.slot(3)), 2, self.left)
 
         def relay(self):
             lo, hi = self.halves
-            self.r_lo.wait_recv()
-            self.rr = send(lo(self.slot(1)), lo(self.slot(2)), self.n + 4, self.right)
-            self.l_hi.wait_recv()
-            self.ll = send(hi(self.slot(3)), hi(self.slot(2)), self.n + 5, self.left)
+            self.arrive(lo(self.slot(1)), 0)
+            self.send(lo(self.slot(1)), lo(self.slot(2)), 3, self.right)
+            self.arrive(hi(self.slot(3)), 1)
+            self.send(hi(self.slot(3)), hi(self.slot(2)), 3, self.left)
 
         def sides(self):
-            self.r_hi.wait_recv()
-            self.l_lo.wait_recv()
+            self.arrive(self.slot(1), 2)
 
         def finish(self):
-            self.rr.wait_recv()
-            self.ll.wait_recv()
-
-    class Scatter:
+            self.arrive(self.slot(2), 3)
+
+    class Scatter(Flow):
         def __init__(self, part, via, arrived, right, left):
+            super().__init__(3, part)
             self.part, self.via, self.arrived = part, via, arrived
             self.right, self.left = right, left
-            self.n = ids(6)
 
         def far(self):
-            self.a = send(self.part.at[1, 0], self.via.at[0], self.n, self.right)
-            self.b = send(self.part.at[1, 1], self.via.at[1], self.n + 1, self.left)
+            self.send(self.part.at[1, 0], self.via.at[0], 0, self.right)
+            self.send(self.part.at[1, 1], self.via.at[1], 1, self.left)
 
         def near(self):
-            self.c = send(self.part.at[2, 1], self.arrived.at[0, 1], self.n + 2, self.right)
-            self.d = send(self.part.at[0, 0], self.arrived.at[1, 0], self.n + 3, self.left)
+            self.send(self.part.at[2, 1], self.arrived.at[0, 1], 2, self.right)
+            self.send(self.part.at[0, 0], self.arrived.at[1, 0], 2, self.left)
 
         def add(self):
             def plus(slot, h):
                 total = self.part[slot, h].astype(F32) + self.via[h].astype(F32)
                 self.part[slot, h] = total.astype(BF16)
 
-            self.a.wait_recv()
+            self.arrive(self.via.at[0], 0)
             plus(2, 0)
-            self.e = send(self.part.at[2, 0], self.arrived.at[0, 0], self.n + 4, self.right)
-            self.b.wait_recv()
+            self.send(self.part.at[2, 0], self.arrived.at[0, 0], 2, self.right)
+            self.arrive(self.via.at[1], 1)
             plus(0, 1)
-            self.g = send(self.part.at[0, 1], self.arrived.at[1, 1], self.n + 5, self.left)
+            self.send(self.part.at[0, 1], self.arrived.at[1, 1], 2, self.left)
 
         def finish(self):
-            for c in (self.c, self.d, self.e, self.g):
-                c.wait_recv()
-
-    class Exchange:
-        def __init__(self, src, slot):
-            self.src, self.slot = src, slot
-            self.n = ids(n_exp - 1)
+            self.arrive(self.arrived, 2)
+
+    class Exchange(Flow):
+        def __init__(self, src, dst):
+            super().__init__(1, src.at[pl.ds(0, n_exp - 1)])
+            self.src, self.dst = src, dst
 
         def start(self):
-            self.copies = [
-                send(
-                    self.src.at[(me + k) % n_exp], self.slot(me), self.n + k - 1,
-                    {"expert": (me + k) % n_exp},
-                )
-                for k in range(1, n_exp)
-            ]
+            for k in range(1, n_exp):
+                peer = (me + k) % n_exp
+                self.send(self.src.at[peer], self.dst.at[me], 0, {"expert": peer})
 
         def finish(self):
-            for c in self.copies:
-                c.wait_recv()
+            self.arrive(self.dst.at[pl.ds(0, n_exp - 1)], 0)
 
     def w_rows(ref, lo, n):
         return ref.at[pl.ds(lo, n), :]
 
     whole_d, whole_h = d // 2, hs // 2
     gather_wg = Gather(
-        wg_ref, lambda s: wg_buf.at[s],
+        wg_ref, wg_buf,
         (lambda r: w_rows(r, 0, whole_d), lambda r: w_rows(r, whole_d, whole_d)), wr, wl,
     )
     gather_wu = Gather(
-        wu_ref, lambda s: wu_buf.at[s],
+        wu_ref, wu_buf,
         (lambda r: w_rows(r, 0, whole_d), lambda r: w_rows(r, whole_d, whole_d)), wr, wl,
     )
     gather_wd = Gather(
-        wd_ref, lambda s: wd_buf.at[s],
+        wd_ref, wd_buf,
         (lambda r: w_rows(r, 0, whole_h), lambda r: w_rows(r, whole_h, whole_h)), wr, wl,
     )
     experts_half = n_exp // 2
@@ -186,16 +186,16 @@
         lambda r: r.at[pl.ds(0, experts_half)],
         lambda r: r.at[pl.ds(experts_half, experts_half)],
     )
-    gather_x = Gather(x_buf.at[0], lambda s: x_buf.at[s], row_halves, tr, tl)
-    gather_g = Gather(g_buf.at[0], lambda s: g_buf.at[s], row_halves, tr, tl)
-    deal_x = Exchange(x_send, lambda e: x_buf.at[0, e])
-    deal_g = Exchange(g_send, lambda e: g_buf.at[0, e])
+    gather_x = Gather(x_buf.at[0], x_buf, row_halves, tr, tl)
+    gather_g = Gather(g_buf.at[0], g_buf, row_halves, tr, tl)
+    deal_x = Exchange(x_send, x_buf.at[0])
+    deal_g = Exchange(g_send, g_buf.at[0])
     scatter_out = Scatter(p_out, via_out, in_out, tr, tl)
     scatter_back = Scatter(p_back, via_back, in_back, tr, tl)
     scatter_gu = Scatter(p_gu, via_gu, in_gu, wr, wl)
     scatter_dn = Scatter(p_dn, via_dn, in_dn, wr, wl)
-    home_out = Exchange(out_send, lambda e: out_home.at[e])
-    home_back = Exchange(back_send, lambda e: back_home.at[e])
+    home_out = Exchange(out_send, out_home)
+    home_back = Exchange(back_send, back_home)
 
     pl.semaphore_wait(barrier, 4 + n_exp - 1)
     gather_wg.start()
@@ -460,8 +460,8 @@
         r = slice(h * hs // 2, (h + 1) * hs // 2)
         dwd_ref[r, :] = own_dn[r, :] + in_dn[0, h].astype(F32) + in_dn[1, h].astype(F32)
 
-    for c in started:
-        c.wait_send()
+    for flow in flows:
+        flow.sent()
 
 
 def write_kernel(*refs):
@@ -481,7 +481,7 @@
     rows = 2 * tok
     hs = gate_weight.shape[2]
     hidden = RING * hs
-    n_copies = 6 * 5 + 6 * 4 + 4 * (n_exp - 1)
+    n_out, n_in = 5 + 4 + 4, 4 * 5 + 3 * 4 + 4
     vmem = pltpu.VMEM
     shapes = [
         vmem((tok, d), BF16),
@@ -508,7 +508,7 @@
     shapes += [vmem((2, 2, n // 2, d), BF16) for n in heights]
     shapes += [vmem((n, d), F32) for n in heights]
     shapes += [vmem((n_exp, cap, d), BF16) for _ in range(4)]
-    shapes += [pltpu.SemaphoreType.DMA((n,)) for n in (n_copies, n_copies, 7)]
+    shapes += [pltpu.SemaphoreType.DMA((n,)) for n in (n_out, n_in, 7)]
     here, away = pl.BlockSpec(memory_space=pltpu.VMEM), pl.BlockSpec(memory_space=pl.ANY)
     results = [
         ((tok, d), BF16), ((tok, d), BF16), ((2, tok), F32),

time: 102 us -> 101 us (level)
    pallas_call x1, Pallas kernels: 99.8 us -> 98.6 us  [per_device(): pl.pallas_call(functools.partial(layer_kernel, n_exp), out_shape=[pltpu.V...]
where the time goes in v4:
time: 101 us
  Pallas kernels  100 us (99%)
    pallas_call x1, Pallas kernels, per_device(): pl.pallas_call(functools.partial(layer_kernel, n_exp), out_shape=[pltpu.V...  98.6 us

profile of v4, /device:TPU:1, one launch (start us, length us, event | category | flops | bytes accessed | tf_op | source)
XLA Modules:
  0.0 101.0 jit_solution(1937748172454831422)
XLA Ops:
  0.6 98.6 %shard_map.118 = (bf16[128,1536]{1,0:T(8,128)(2,1)S(1)}, bf16[128,1536]{1,0:T(8,128)(2,1)S(1)}, f32[2,128]{1,0:T(2,128)S(1)}, f32[1536,128]{1,0:T(8,128)S(1)}, f...) custom-call(bf16[128,1536]{1,0:T(8,128)(2,1)} %tok_hbm.1, f32[2,128]{1,0:T(2,128)} %bitcast.12, s32[2,128]{1,0:T(2,128)} %bitcast.13, ...), custom_call_target="tpu_custom_call" | custom-call | tf_op jit(solution)/shard_map/pallas_call | solution.py:517
  99.3 1.7 %shard_map.119 = (bf16[128,1536]{1,0:T(8,128)(2,1)}, bf16[128,1536]{1,0:T(8,128)(2,1)}, f32[2,128]{1,0:T(2,128)}, f32[1536,128]{1,0:T(8,128)}, f32[1536,128]{1,0:T(8,128)}, /*index=5*/f32[128,1536]{1,0:T(8,128)}) custom-call(bf16[128,1536]{1,0:T(8,128)(2,1)S(1)} %get-tuple-element.18.refs_0_, bf16[128,1536]{1,0:T(8,128)(2,1)S(1)} %get-tuple-element.19.refs_1_, ...), custom_call_target="tpu_custom_call" | custom-call | tf_op jit(solution)/shard_map/pallas_call | solution.py:530

commit v5 on v4

--- a/solution.py
+++ b/solution.py
@@ -60,8 +60,9 @@
         pltpu.make_async_copy(src, dst, load_sem.at[n])
         for n, (src, dst) in enumerate(
             [
-                (ids_hbm, ids_ref), (gp_hbm, gp_ref), (tok_hbm, tok_ref), (cot_hbm, cot_ref),
-                (wg_ref, wg_buf.at[0]), (wu_ref, wu_buf.at[0]), (wd_ref, wd_buf.at[0]),
+                (wg_ref, wg_buf.at[0]), (ids_hbm, ids_ref), (gp_hbm, gp_ref),
+                (tok_hbm, tok_ref), (wu_ref, wu_buf.at[0]), (wd_ref, wd_buf.at[0]),
+                (cot_hbm, cot_ref),
             ]
         )
     ]
@@ -170,15 +171,15 @@
 
     whole_d, whole_h = d // 2, hs // 2
     gather_wg = Gather(
-        wg_ref, wg_buf,
+        wg_buf.at[0], wg_buf,
         (lambda r: w_rows(r, 0, whole_d), lambda r: w_rows(r, whole_d, whole_d)), wr, wl,
     )
     gather_wu = Gather(
-        wu_ref, wu_buf,
+        wu_buf.at[0], wu_buf,
         (lambda r: w_rows(r, 0, whole_d), lambda r: w_rows(r, whole_d, whole_d)), wr, wl,
     )
     gather_wd = Gather(
-        wd_ref, wd_buf,
+        wd_buf.at[0], wd_buf,
         (lambda r: w_rows(r, 0, whole_h), lambda r: w_rows(r, whole_h, whole_h)), wr, wl,
     )
     experts_half = n_exp // 2
@@ -198,12 +199,12 @@
     home_back = Exchange(back_send, back_home)
 
     pl.semaphore_wait(barrier, 4 + n_exp - 1)
-    gather_wg.start()
-    gather_wu.start()
-    gather_wd.start()
-
-    loads[0].wait()
+    for load, gather in ((0, gather_wg), (4, gather_wu), (5, gather_wd)):
+        loads[load].wait()
+        gather.start()
+
     loads[1].wait()
+    loads[2].wait()
     lane = lax.broadcasted_iota(jnp.int32, (tok, rows), 1)
     expert_of, slot_of = lane // cap, lane % cap
     token = lax.broadcasted_iota(jnp.int32, (tok, tok), 0)
@@ -235,7 +236,7 @@
         x_send[:, :, c] = sent.astype(BF16).reshape(n_exp, cap, tile)
         return 0
 
-    loads[2].wait()
+    loads[3].wait()
     lax.fori_loop(0, n_tiles, deal_tile, 0)
     deal_x.start()
     x_buf[0, me] = x_send[me]
@@ -253,7 +254,7 @@
         g_send[:, :, c] = sent.astype(BF16).reshape(n_exp, cap, tile)
         return 0
 
-    loads[3].wait()
+    loads[6].wait()
     lax.fori_loop(0, n_tiles, deal_grad_tile, 0)
     deal_g.start()
     g_buf[0, me] = g_send[me]
@@ -366,8 +367,6 @@
                 experts_half, cap, d
             )
 
-    for load in loads[4:]:
-        load.wait()
     for gather in (gather_wg, gather_wu):
         gather.sides()
         gather.finish()

time: 101 us -> 101 us (level)
  no operation moved by 1% of the time
where the time goes in v5:
time: 101 us
  Pallas kernels  100 us (99%)
    pallas_call x1, Pallas kernels, per_device(): pl.pallas_call(functools.partial(layer_kernel, n_exp), out_shape=[pltpu.V...  98.4 us

profile of v5, /device:TPU:1, one launch (start us, length us, event | category | flops | bytes accessed | tf_op | source)
XLA Modules:
  0.0 100.8 jit_solution(16578743948507350736)
XLA Ops:
  0.6 98.4 %shard_map.118 = (bf16[128,1536]{1,0:T(8,128)(2,1)S(1)}, bf16[128,1536]{1,0:T(8,128)(2,1)S(1)}, f32[2,128]{1,0:T(2,128)S(1)}, f32[1536,128]{1,0:T(8,128)S(1)}, f...) custom-call(bf16[128,1536]{1,0:T(8,128)(2,1)} %tok_hbm.1, f32[2,128]{1,0:T(2,128)} %bitcast.12, s32[2,128]{1,0:T(2,128)} %bitcast.13, ...), custom_call_target="tpu_custom_call" | custom-call | tf_op jit(solution)/shard_map/pallas_call | solution.py:516
  99.1 1.7 %shard_map.119 = (bf16[128,1536]{1,0:T(8,128)(2,1)}, bf16[128,1536]{1,0:T(8,128)(2,1)}, f32[2,128]{1,0:T(2,128)}, f32[1536,128]{1,0:T(8,128)}, f32[1536,128]{1,0:T(8,128)}, /*index=5*/f32[128,1536]{1,0:T(8,128)}) custom-call(bf16[128,1536]{1,0:T(8,128)(2,1)S(1)} %get-tuple-element.18.refs_0_, bf16[128,1536]{1,0:T(8,128)(2,1)S(1)} %get-tuple-element.19.refs_1_, ...), custom_call_target="tpu_custom_call" | custom-call | tf_op jit(solution)/shard_map/pallas_call | solution.py:529

commit v6 on v5

--- a/solution.py
+++ b/solution.py
@@ -78,8 +78,9 @@
         return first
 
     class Flow:
-        def __init__(self, n_recv, bytes_out):
-            self.out, self.into = take(0, 1), take(1, n_recv)
+        def __init__(self, n_recv, bytes_out, into=None):
+            self.out = take(0, 1)
+            self.into = take(1, n_recv) if into is None else into
             self.bytes_out = bytes_out
             flows.append(self)
 
@@ -99,24 +100,39 @@
             self.descriptor(self.bytes_out, self.bytes_out, 0, tr).wait_send()
 
     class Gather(Flow):
-        def __init__(self, own, buf, halves, right, left):
-            super().__init__(4, buf.at[pl.ds(1, RING - 1)])
+        def __init__(self, own, buf, halves, right, left, into=None):
+            super().__init__(4, buf.at[pl.ds(1, RING - 1)], into)
             self.own, self.slot, self.halves = own, lambda k: buf.at[k], halves
             self.right, self.left = right, left
 
         def start(self):
+            self.start_first()
+            self.start_second()
+
+        def start_first(self):
             lo, hi = self.halves
             self.send(lo(self.own), lo(self.slot(1)), 0, self.right)
             self.send(hi(self.own), hi(self.slot(3)), 1, self.left)
+
+        def start_second(self):
+            lo, hi = self.halves
             self.send(hi(self.own), hi(self.slot(1)), 2, self.right)
             self.send(lo(self.own), lo(self.slot(3)), 2, self.left)
+
+        def relay_right(self):
+            lo, _ = self.halves
+            self.send(lo(self.slot(1)), lo(self.slot(2)), 3, self.right)
+
+        def relay_left(self):
+            _, hi = self.halves
+            self.send(hi(self.slot(3)), hi(self.slot(2)), 3, self.left)
 
         def relay(self):
             lo, hi = self.halves
             self.arrive(lo(self.slot(1)), 0)
-            self.send(lo(self.slot(1)), lo(self.slot(2)), 3, self.right)
+            self.relay_right()
             self.arrive(hi(self.slot(3)), 1)
-            self.send(hi(self.slot(3)), hi(self.slot(2)), 3, self.left)
+            self.relay_left()
 
         def sides(self):
             self.arrive(self.slot(1), 2)
@@ -177,11 +193,14 @@
     gather_wu = Gather(
         wu_buf.at[0], wu_buf,
         (lambda r: w_rows(r, 0, whole_d), lambda r: w_rows(r, whole_d, whole_d)), wr, wl,
+        gather_wg.into,
     )
     gather_wd = Gather(
         wd_buf.at[0], wd_buf,
         (lambda r: w_rows(r, 0, whole_h), lambda r: w_rows(r, whole_h, whole_h)), wr, wl,
+        gather_wg.into,
     )
+    weights = (gather_wg, gather_wu, gather_wd)
     experts_half = n_exp // 2
     row_halves = (
         lambda r: r.at[pl.ds(0, experts_half)],
@@ -199,9 +218,11 @@
     home_back = Exchange(back_send, back_home)
 
     pl.semaphore_wait(barrier, 4 + n_exp - 1)
-    for load, gather in ((0, gather_wg), (4, gather_wu), (5, gather_wd)):
+    for load, gather in zip((0, 4, 5), weights):
         loads[load].wait()
-        gather.start()
+        gather.start_first()
+    for gather in weights:
+        gather.start_second()
 
     loads[1].wait()
     loads[2].wait()
@@ -263,11 +284,15 @@
     wu = [wu_buf.at[s] for s in range(RING)]
     wd = [wd_buf.at[s] for s in range(RING)]
 
-    gather_wg.relay()
-    gather_wu.relay()
+    halves_in = wg_buf.at[pl.ds(1, 3), pl.ds(0, whole_d)]
+    gather_wg.arrive(halves_in, 0)
+    for gather in weights:
+        gather.relay_right()
+    gather_wg.arrive(halves_in, 1)
+    for gather in weights:
+        gather.relay_left()
     deal_x.finish()
     gather_x.start()
-    gather_wd.relay()
     deal_g.finish()
     gather_x.relay()
     gather_g.start()
@@ -367,17 +392,15 @@
                 experts_half, cap, d
             )
 
-    for gather in (gather_wg, gather_wu):
-        gather.sides()
-        gather.finish()
+    blocks_in = wg_buf.at[pl.ds(1, 3)]
+    for n in (2, 3):
+        gather_wg.arrive(blocks_in, n)
     forward(0)
     gather_x.sides()
     both_sides(forward)
     gather_x.finish()
     forward(2)
     gather_g.relay()
-    gather_wd.sides()
-    gather_wd.finish()
     out_part(2)
     scatter_out.far()
     out_part(1)
@@ -480,7 +503,7 @@
     rows = 2 * tok
     hs = gate_weight.shape[2]
     hidden = RING * hs
-    n_out, n_in = 5 + 4 + 4, 4 * 5 + 3 * 4 + 4
+    n_out, n_in = 5 + 4 + 4, 4 * 3 + 3 * 4 + 4
     vmem = pltpu.VMEM
     shapes = [
         vmem((tok, d), BF16),

time: 101 us -> 101 us (level)
  no operation moved by 1% of the time
where the time goes in v6:
time: 101 us
  Pallas kernels  100 us (99%)
    pallas_call x1, Pallas kernels, per_device(): pl.pallas_call(functools.partial(layer_kernel, n_exp), out_shape=[pltpu.V...  98.3 us

profile of v6, /device:TPU:1, one launch (start us, length us, event | category | flops | bytes accessed | tf_op | source)
XLA Modules:
  0.0 100.7 jit_solution(725807063553264216)
XLA Ops:
  0.6 98.3 %shard_map.118 = (bf16[128,1536]{1,0:T(8,128)(2,1)S(1)}, bf16[128,1536]{1,0:T(8,128)(2,1)S(1)}, f32[2,128]{1,0:T(2,128)S(1)}, f32[1536,128]{1,0:T(8,128)S(1)}, f...) custom-call(bf16[128,1536]{1,0:T(8,128)(2,1)} %tok_hbm.1, f32[2,128]{1,0:T(2,128)} %bitcast.12, s32[2,128]{1,0:T(2,128)} %bitcast.13, ...), custom_call_target="tpu_custom_call" | custom-call | tf_op jit(solution)/shard_map/pallas_call | solution.py:539
  99.0 1.7 %shard_map.119 = (bf16[128,1536]{1,0:T(8,128)(2,1)}, bf16[128,1536]{1,0:T(8,128)(2,1)}, f32[2,128]{1,0:T(2,128)}, f32[1536,128]{1,0:T(8,128)}, f32[1536,128]{1,0:T(8,128)}, /*index=5*/f32[128,1536]{1,0:T(8,128)}) custom-call(bf16[128,1536]{1,0:T(8,128)(2,1)S(1)} %get-tuple-element.18.refs_0_, bf16[128,1536]{1,0:T(8,128)(2,1)S(1)} %get-tuple-element.19.refs_1_, ...), custom_call_target="tpu_custom_call" | custom-call | tf_op jit(solution)/shard_map/pallas_call | solution.py:552

commit v7 on v5

--- a/solution.py
+++ b/solution.py
@@ -256,7 +256,6 @@
 
     loads[6].wait()
     lax.fori_loop(0, n_tiles, deal_grad_tile, 0)
-    deal_g.start()
     g_buf[0, me] = g_send[me]
 
     wg = [wg_buf.at[s] for s in range(RING)]
@@ -264,6 +263,7 @@
     wd = [wd_buf.at[s] for s in range(RING)]
 
     gather_wg.relay()
+    deal_g.start()
     gather_wu.relay()
     deal_x.finish()
     gather_x.start()

time: 101 us -> 101 us (level)
  no operation moved by 1% of the time
where the time goes in v7:
time: 101 us
  Pallas kernels  100 us (99%)
    pallas_call x1, Pallas kernels, per_device(): pl.pallas_call(functools.partial(layer_kernel, n_exp), out_shape=[pltpu.V...  98.4 us

profile of v7, /device:TPU:1, one launch (start us, length us, event | category | flops | bytes accessed | tf_op | source)
XLA Modules:
  0.0 100.8 jit_solution(18127290190426613987)
XLA Ops:
  0.6 98.4 %shard_map.118 = (bf16[128,1536]{1,0:T(8,128)(2,1)S(1)}, bf16[128,1536]{1,0:T(8,128)(2,1)S(1)}, f32[2,128]{1,0:T(2,128)S(1)}, f32[1536,128]{1,0:T(8,128)S(1)}, f...) custom-call(bf16[128,1536]{1,0:T(8,128)(2,1)} %tok_hbm.1, f32[2,128]{1,0:T(2,128)} %bitcast.12, s32[2,128]{1,0:T(2,128)} %bitcast.13, ...), custom_call_target="tpu_custom_call" | custom-call | tf_op jit(solution)/shard_map/pallas_call | solution.py:516
  99.1 1.7 %shard_map.119 = (bf16[128,1536]{1,0:T(8,128)(2,1)}, bf16[128,1536]{1,0:T(8,128)(2,1)}, f32[2,128]{1,0:T(2,128)}, f32[1536,128]{1,0:T(8,128)}, f32[1536,128]{1,0:T(8,128)}, /*index=5*/f32[128,1536]{1,0:T(8,128)}) custom-call(bf16[128,1536]{1,0:T(8,128)(2,1)S(1)} %get-tuple-element.18.refs_0_, bf16[128,1536]{1,0:T(8,128)(2,1)S(1)} %get-tuple-element.19.refs_1_, ...), custom_call_target="tpu_custom_call" | custom-call | tf_op jit(solution)/shard_map/pallas_call | solution.py:529
